TPU v7x, 32 devices: a whole 2x2x4 slice. The times are simulated.
32 devices in a mesh: wave: 8 (over z, x), lev: 4 (over y, core).
Axes of the slice: x: 2, y: 2, z: 4, core: 2. Of those that a mesh axis runs over, the one named last changes fastest.
Arguments:
- spectral: bfloat16 [32, 3, 2, 72, 192], P('wave', None, None, None, 'lev'), may hold values from -6 to 6
- vertical_ops: bfloat16 [3, 72, 72], replicated, may hold values from -0.75 to 0.75
- legendre: bfloat16 [32, 2, 4, 192], P('wave'), may hold values from -0.125 to 0.125
- legendre_slope: bfloat16 [32, 2, 4, 192], P('wave'), may hold values from -4.1875 to 4.1875
- sine_lat: float32 [4], replicated, may hold values from 0.05 to 0.85
- pair_map: int32 [32], replicated, may hold values from 0 to 31, each once
- lon_counts: int32 [8], replicated, may hold values from 640 to 5120, as said below
Outputs:
- tendency: float32 [72, 8, 5120], P('lev', 'wave')
Inputs may be any that keep to these rules, and one draw needn't show every extreme that they name: `pair_map`: each pair number appears once. `lon_counts`: every count is a multiple of 64; row 4 + j has the count of row j; some row has 5120.
All inputs are finite; a program needn't handle non-finite values.
Results may differ from a plain program's by a relative error of at most 0.0067.
Values may be sent and summed in bfloat16 or wider, within the bound.
No kernel may reach another device: no remote copies, remote signals or barrier semaphores. Data moves between devices by JAX's collectives and lax.ppermute only.
A program may use at most 64 MiB of HBM per device.

v0:
```python
import math

import jax
import jax.numpy as jnp
from jax import lax
from jax.sharding import PartitionSpec as P

NLON = 5120


def make_masks(pair_numbers, total_waves, full_width):
    half_width = full_width // 2
    positions = jnp.arange(full_width, dtype=jnp.int32)
    upper_half = positions >= half_width
    offset = jnp.where(upper_half, positions - half_width, positions)
    pair_col = pair_numbers[:, None]
    first_count = jnp.where(
        upper_half[None, :], (total_waves - pair_col) // 2, (total_waves - pair_col + 1) // 2
    )
    second = jnp.where(upper_half[None, :], (pair_col + 1) // 2, (pair_col + 2) // 2)
    first_mask = (offset[None, :] < first_count).astype(jnp.float32)
    second_mask = (
        (offset[None, :] >= first_count) & (offset[None, :] < first_count + second)
    ).astype(jnp.float32)
    return jnp.stack([first_mask, second_mask], axis=1)


def wave_numbers(pair_numbers, total_waves):
    return jnp.stack([pair_numbers, total_waves - 1 - pair_numbers], axis=1).reshape(-1)


def angle_table(waves, offsets, lon_count):
    products = waves[:, None] * offsets[None, :] % lon_count
    angles = 2.0 * math.pi * products.astype(jnp.float32) / lon_count.astype(jnp.float32)
    return (jnp.cos(angles), jnp.sin(angles))


def basis_block(waves, lon_count, start_col, block_width, total_waves):
    coarse_cols = start_col + 64 * jnp.arange(block_width // 64, dtype=jnp.int32)
    fine_cols = jnp.arange(64, dtype=jnp.int32)
    coarse_cos, coarse_sin = angle_table(waves, coarse_cols, lon_count)
    fine_cos, fine_sin = angle_table(waves, fine_cols, lon_count)
    wave_count = waves.shape[0]
    cosine = (
        coarse_cos[:, :, None] * fine_cos[:, None, :]
        - coarse_sin[:, :, None] * fine_sin[:, None, :]
    ).reshape(wave_count, block_width)
    sine_part = (
        coarse_sin[:, :, None] * fine_cos[:, None, :]
        + coarse_cos[:, :, None] * fine_sin[:, None, :]
    ).reshape(wave_count, block_width)
    columns = start_col + jnp.arange(block_width, dtype=jnp.int32)
    inside = (columns < lon_count).astype(jnp.float32)[None, :]
    cosine = cosine * inside
    sine_part = sine_part * inside
    weight = jnp.where(waves == 0, 1.0, jnp.where(2 * waves < lon_count, 2.0, 0.0)).astype(
        jnp.float32
    )
    plain_basis = jnp.concatenate([weight[:, None] * cosine, -weight[:, None] * sine_part], axis=0)
    factor = (waves.astype(jnp.float32) * weight / total_waves)[:, None]
    turning = jnp.concatenate([-factor * sine_part, -factor * cosine], axis=0)
    return (plain_basis.astype(jnp.bfloat16), turning.astype(jnp.bfloat16))


def assemble(hemisphere_parts):
    stacked = []
    for north_part, south_part in hemisphere_parts:
        joined = jnp.concatenate([north_part, south_part], axis=-1)
        reordered = jnp.transpose(joined, (2, 4, 1, 0, 3))
        stacked.append(
            reordered.reshape(reordered.shape[0], reordered.shape[1], reordered.shape[2], -1)
        )
    return jnp.stack(stacked, axis=2)


def per_device(spectral, vertical_ops, legendre, legendre_slope, sine_lat, pair_map, lon_counts):
    pair_count = spectral.shape[0]
    local_width = spectral.shape[4]
    full_width = local_width * lax.axis_size("lev")
    half_width = full_width // 2
    total_waves = 2 * pair_map.shape[0]
    vertical = jnp.einsum(
        "fkl,pfcln->pfckn", vertical_ops, spectral, preferred_element_type=jnp.float32
    ).astype(jnp.bfloat16)
    own_pairs = lax.dynamic_slice_in_dim(pair_map, lax.axis_index("wave") * pair_count, pair_count)
    masks = make_masks(own_pairs, total_waves, full_width)
    basis_table = (legendre * masks[:, :, None, :]).astype(jnp.bfloat16)
    slope_table = (legendre_slope * masks[:, :, None, :]).astype(jnp.bfloat16)
    transposed = lax.all_to_all(vertical, "lev", split_axis=3, concat_axis=4, tiled=True)
    even_part = jnp.einsum(
        "pfcln,pwjn->pfclwj",
        transposed[..., :half_width],
        basis_table[..., :half_width],
        preferred_element_type=jnp.float32,
    )
    odd_part = jnp.einsum(
        "pfcln,pwjn->pfclwj",
        transposed[..., half_width:],
        basis_table[..., half_width:],
        preferred_element_type=jnp.float32,
    )
    even_slope = jnp.einsum(
        "pcln,pwjn->pclwj",
        transposed[:, 2, ..., :half_width],
        slope_table[..., :half_width],
        preferred_element_type=jnp.float32,
    )
    odd_slope = jnp.einsum(
        "pcln,pwjn->pclwj",
        transposed[:, 2, ..., half_width:],
        slope_table[..., half_width:],
        preferred_element_type=jnp.float32,
    )
    legendre_sums = assemble(
        [
            (even_part[:, 0] + odd_part[:, 0], even_part[:, 0] - odd_part[:, 0]),
            (even_part[:, 1] + odd_part[:, 1], even_part[:, 1] - odd_part[:, 1]),
            (even_slope + odd_slope, odd_slope - even_slope),
            (even_part[:, 2] + odd_part[:, 2], even_part[:, 2] - odd_part[:, 2]),
        ]
    )
    fourier = legendre_sums.astype(jnp.bfloat16)
    row_index = lax.axis_index("wave")
    lon_count = lon_counts[row_index]
    rows_sine = jnp.concatenate([sine_lat, -sine_lat])
    sine_row = rows_sine[row_index]
    waves = wave_numbers(pair_map, total_waves)
    received = lax.all_to_all(fourier, "wave", split_axis=1, concat_axis=4, tiled=True)
    level_count = received.shape[0]
    coeffs = received[:, 0].reshape(level_count, 4, 2 * total_waves)
    three_fields = coeffs[:, 0:3].reshape(level_count * 3, 2 * total_waves)
    turning_coeffs = coeffs[:, 3]

    def block_step(block_index, output):
        plain_basis, turning = basis_block(waves, lon_count, block_index * 512, 512, total_waves)
        grid_values = jnp.dot(
            three_fields, plain_basis, preferred_element_type=jnp.float32
        ).reshape(level_count, 3, 512)
        zonal_slope = jnp.dot(turning_coeffs, turning, preferred_element_type=jnp.float32)
        tendency = -(
            grid_values[:, 0] * zonal_slope / (1.0 - sine_row * sine_row)
            + grid_values[:, 1] * grid_values[:, 2] / total_waves
        )
        return lax.dynamic_update_slice_in_dim(output, tendency, block_index * 512, 1)

    output = lax.fori_loop(0, NLON // 512, block_step, jnp.zeros((level_count, NLON), jnp.float32))
    return output[:, None, :]


def solution(mesh):
    placed = (
        P("wave", None, None, None, "lev"),
        P(),
        P("wave", None, None, None),
        P("wave", None, None, None),
        P(),
        P(),
        P(),
    )
    return jax.shard_map(
        per_device, mesh=mesh, in_specs=placed, out_specs=P("lev", "wave", None), check_vma=False
    )
```

profile of v0, /device:TPU:0, one launch (start us, length us, event | category | flops | bytes accessed | tf_op | source)
XLA Modules:
  0.0 64.4 jit_solution(4816560327908192289)
XLA Ops:
  0.0 0.8 %copy-done = bf16[3,72,72]{2,1,0:T(8,128)(2,1)S(1)} copy-done((bf16[3,72,72]{2,1,0:T(8,128)(2,1)S(1)}, bf16[3,72,72]{2,1,0:T(8,128)(2,1)}, u32[]{:S(2)}) %copy-start) | copy-done | bytes 31128
  0.8 1.2 %fusion.36 = bf16[4,3,2,72,48]{3,4,2,0,1:T(8,128)(2,1)S(1)} fusion(bf16[4,3,2,72,48]{3,4,2,1,0:T(8,128)(2,1)} %param.9, bf16[3,72,72]{2,1,0:T(8,128)(2,1)S(1)} %copy-done), kind=kOutput, calls=%fused_computation.56 | convolution fusion | flops 12026880 | bytes 362880 | tf_op jit(solution)/shard_map/fkl,pfcln->pfckn/dot_general | solution.py:82
  2.5 1.3 %reshape.613 = bf16[4,2,10368]{2,1,0:T(2,128)(2,1)} reshape(bf16[72,3,4,2,48]{4,3,2,1,0:T(2,128)(2,1)S(1)} %bitcast.188) | data formatting | bytes 331776
  3.8 4.3 %all-to-all-start = ((bf16[4,2,10368]{2,1,0:T(2,128)(2,1)}), bf16[4,2,10368]{2,1,0:T(2,128)(2,1)S(1)}, u32[]{:S(2)}, u32[]{:S(2)}) async-start(bf16[4,2,10368]{2,1,0:T(2,128)(2,1)} %reshape.613), calls=%async_computation | async-start | bytes 331776 | tf_op jit(solution)/shard_map/all_to_all | solution.py:89
  8.1 0.6 %copy-done.4 = s32[32]{0:T(128)S(1)} copy-done((s32[32]{0:T(128)S(1)}, s32[32]{0:T(128)}, u32[]{:S(2)}) %copy-start.4) | copy-done | bytes 152
  10.3 2.8 %all-to-all-done = bf16[4,2,10368]{2,1,0:T(2,128)(2,1)S(1)} async-done(((bf16[4,2,10368]{2,1,0:T(2,128)(2,1)}), bf16[4,2,10368]{2,1,0:T(2,128)(2,1)S(1)}, u32[]{:S(2)}, u32[]{:S(2)}) %all-to-all-start) | async-done | bytes 165920 | tf_op jit(solution)/shard_map/all_to_all | solution.py:89
  16.0 0.8 %reshape.615 = bf16[8,2,576]{2,1,0:T(2,128)(2,1)} reshape(bf16[8,4,2,8,18]{4,3,2,1,0:T(8,128)(2,1)S(1)} %bitcast.191) | data formatting | bytes 36864
  16.8 6.3 %all-to-all-start.1 = ((bf16[8,2,576]{2,1,0:T(2,128)(2,1)}), bf16[8,2,576]{2,1,0:T(2,128)(2,1)S(1)}, u32[]{:S(2)}, u32[]{:S(2)}) async-start(bf16[8,2,576]{2,1,0:T(2,128)(2,1)} %reshape.615), calls=%async_computation.1 | async-start | bytes 40960 | tf_op jit(solution)/shard_map/all_to_all | solution.py:128
  23.3 0.7 %copy-done.6 = s32[8]{0:T(128)S(1)} copy-done((s32[8]{0:T(128)S(1)}, s32[8]{0:T(128)}, u32[]{:S(2)}) %copy-start.6) | copy-done | bytes 56
  27.1 0.7 %dynamic_slice.11 = f32[1]{0:T(128)} dynamic-slice(f32[8]{0:T(128)S(1)} %pad_maximum_fusion.1, s32[]{:T(128)S(6)} %select_n.182), dynamic_slice_sizes={1} | dynamic-slice | bytes 12 | tf_op jit(solution)/shard_map/dynamic_slice | solution.py:126
  30.5 32.9 %while.16 = (s32[]{:T(128)}, f32[18,5120]{1,0:T(8,128)S(1)}, s32[64]{0:T(128)S(1)}, s32[]{:T(128)}, s32[32,2]{1,0:T(8,128)}, /*index=5*/s32[]{:T(128)}, pred[]{:...) while((s32[]{:T(128)}, f32[18,5120]{1,0:T(8,128)S(1)}, ...), condition=%wide.wide.region_1.2_spmd, body=%wide.wide.region_0.1_spmd.sunk | while | flops 10593878 | bytes 2394677 | solution.py:146
  30.5 0.6 fusion.93
  31.2 0.6 fusion.94
  33.8 0.6 fusion.93
  34.4 0.6 fusion.94
  37.1 0.6 fusion.93
  40.4 0.6 fusion.93
  43.7 0.6 fusion.93
  47.0 0.6 fusion.93
  50.3 0.6 fusion.93
  53.5 0.6 fusion.93
  56.8 0.6 fusion.93
  60.1 0.6 fusion.93
  63.4 1.0 %broadcast_in_dim.109 = f32[18,1,5120]{2,1,0:T(1,128)} reshape(f32[18,5120]{1,0:T(8,128)S(1)} %get-tuple-element.220) | data formatting | bytes 737280 | tf_op jit(solution)/shard_map/broadcast_in_dim | solution.py:147
  (207 shorter events, 31.8 us)
Async XLA Ops:
  0.0 0.8 %copy-start = (bf16[3,72,72]{2,1,0:T(8,128)(2,1)S(1)}, bf16[3,72,72]{2,1,0:T(8,128)(2,1)}, u32[]{:S(2)}) copy-start(bf16[3,72,72]{2,1,0:T(8,128)(2,1)} %param.10) | copy-start | bytes 93316
  3.8 9.2 %all-to-all-start = ((bf16[4,2,10368]{2,1,0:T(2,128)(2,1)}), bf16[4,2,10368]{2,1,0:T(2,128)(2,1)S(1)}, u32[]{:S(2)}, u32[]{:S(2)}) async-start(bf16[4,2,10368]{2,1,0:T(2,128)(2,1)} %reshape.613), calls=%async_computation | async-start | bytes 331776 | tf_op jit(solution)/shard_map/all_to_all | solution.py:89
  8.1 0.7 %copy-start.4 = (s32[32]{0:T(128)S(1)}, s32[32]{0:T(128)}, u32[]{:S(2)}) copy-start(s32[32]{0:T(128)} %param.14) | copy-start | bytes 388
  8.8 0.7 %copy-start.3 = (bf16[4,2,4,192]{3,2,1,0:T(4,128)(2,1)S(1)}, bf16[4,2,4,192]{3,2,1,0:T(4,128)(2,1)}, u32[]{:S(2)}) copy-start(bf16[4,2,4,192]{3,2,1,0:T(4,128)(2,1)} %param.11) | copy-start | bytes 36868
  8.9 0.7 %copy-start.2 = (bf16[4,2,4,192]{3,2,1,0:T(4,128)(2,1)S(1)}, bf16[4,2,4,192]{3,2,1,0:T(4,128)(2,1)}, u32[]{:S(2)}) copy-start(bf16[4,2,4,192]{3,2,1,0:T(4,128)(2,1)} %param.12) | copy-start | bytes 36868
  9.6 0.7 %copy-start.5 = (f32[4]{0:T(128)S(1)}, f32[4]{0:T(128)}, u32[]{:S(2)}) copy-start(f32[4]{0:T(128)} %param.13) | copy-start | bytes 52
  16.8 12.9 %all-to-all-start.1 = ((bf16[8,2,576]{2,1,0:T(2,128)(2,1)}), bf16[8,2,576]{2,1,0:T(2,128)(2,1)S(1)}, u32[]{:S(2)}, u32[]{:S(2)}) async-start(bf16[8,2,576]{2,1,0:T(2,128)(2,1)} %reshape.615), calls=%async_computation.1 | async-start | bytes 40960 | tf_op jit(solution)/shard_map/all_to_all | solution.py:128
  23.3 0.7 %copy-start.6 = (s32[8]{0:T(128)S(1)}, s32[8]{0:T(128)}, u32[]{:S(2)}) copy-start(s32[8]{0:T(128)} %param.15) | copy-start | bytes 100
  25.9 0.6 copy-start.1
where the time goes:
time: 65 us; the launch traced here: 64.4 us
  other arithmetic  24.4 us (38%)
  local copies, waits for them, and re-layouts  16.5 us (25%)
  starting transfers between devices  10.6 us (16%)
  matrix products  5.13 us (8%)
  between operations  3.48 us (5%)
  waiting for transfers between devices  3.31 us (5%)
  loops' own time  1.02 us (2%)
    cos x20, other arithmetic, angle_table(): return (jnp.cos(angles), jnp.sin(angles))  7.99 us
    unnamed x18, local copies, waits for them, and re-layouts  6.62 us
    neg x10, other arithmetic, basis_block(): -weight[:, None] * sine_part  6.37 us
    convert_element_type x10, other arithmetic, basis_block(): inside = (columns < lon_count).astype(jnp.float32)[None, :]  6.35 us
    all_to_all x1, starting transfers between devices, per_device(): lax.all_to_all(fourier, 'wave', split_axis=1, concat_axis=4, tiled=True)  6.34 us
    all_to_all x1, starting transfers between devices, per_device(): lax.all_to_all(vertical, 'lev', split_axis=3, concat_axis=4, tiled=True)  4.26 us
    all_to_all x1, waiting for transfers between devices, per_device(): lax.all_to_all(vertical, 'lev', split_axis=3, concat_axis=4, tiled=True)  2.77 us
    add x10, other arithmetic, basis_block(): coarse_sin[:, :, None] * fine_cos[:, None, :]  2.05 us
  transfers between devices with their start and end apart: 2, of which 2 were waited for; matrix products, arithmetic and copies ran while one was open for 3% of the time, Pallas kernels for 0%

commit v1 on v0

v1 whole, which is shorter than its diff:
```python
import functools
import math

import jax
import jax.numpy as jnp
from jax import lax
from jax.experimental import pallas as pl
from jax.experimental.pallas import tpu as pltpu
from jax.sharding import PartitionSpec as P

NLON = 5120
FIELDS = 4
LANES = 128
COLS = 512

F32 = jnp.float32
BF16 = jnp.bfloat16
NT = (((1,), (1,)), ((), ()))
TN = (((0,), (0,)), ((), ()))


def dot(a, b, dims=(((1,), (0,)), ((), ()))):
    return lax.dot_general(a, b, dims, preferred_element_type=F32)


def iota(shape, dim):
    return lax.broadcasted_iota(jnp.int32, shape, dim)


def row_pairs(pair_ref, first, count, shape):
    slot = iota(shape, 0) // 2
    numbers = jnp.zeros(shape, jnp.int32)
    for index in range(count):
        numbers = jnp.where(slot == index, pair_ref[first + index], numbers)
    return numbers


def partial_kernel(
    sizes, pair_ref, spectral_ref, ops_ref, legendre_ref, slope_ref, send_ref, table_ref
):
    pairs, level_ranks, levels_out, pad, total_waves = sizes
    _, fields, parts, width, levels = spectral_ref.shape
    _, orders, lats, full = legendre_ref.shape
    half = full // 2
    rank = lax.axis_index("lev")
    first_pair = lax.axis_index("wave") * pairs
    sub = pairs * orders
    rows = lats * parts * sub
    cols = pairs * parts * width

    for t, ref in enumerate((legendre_ref, slope_ref)):
        for s in range(pairs):
            for w in range(orders):
                base = ((t * pairs + s) * orders + w) * lats
                table_ref[base : base + lats, :] = ref[s, w].astype(F32)
    table = table_ref[...].astype(BF16)

    r = iota((2 * rows, 2 * sub * lats), 0)
    t, j, sw = r // rows, (r % rows) // (parts * sub), r % sub
    wanted = (t * sub + sw) * lats + j
    pick = (iota(r.shape, 1) == wanted).astype(F32).astype(BF16)
    picked = dot(pick, table).astype(BF16)
    shape = (full, cols)
    place = (iota(shape, 0) == rank * width + iota(shape, 1) % width).astype(F32).astype(BF16)
    spread = dot(picked, place)

    shape = (rows, cols)
    r, col = iota(shape, 0), iota(shape, 1)
    part, slot, order = (r // sub) % parts, (r % sub) // orders, r % orders
    number = jnp.zeros(shape, jnp.int32)
    for s in range(pairs):
        number = jnp.where(slot == s, pair_ref[first_pair + s], number)
    position = rank * width + col % width
    upper = (position >= half).astype(jnp.int32)
    offset = position - half * upper
    count0 = (total_waves - number + 1 - upper) >> 1
    count1 = (number + 2 - upper) >> 1
    low = jnp.where(order == 0, 0, count0)
    high = jnp.where(order == 0, count0, count0 + count1)
    block = col // width
    keep = (offset >= low) & (offset < high) & (block == slot * parts + part)
    basis = jnp.where(keep, spread[:rows], 0.0).astype(BF16)
    slope_basis = jnp.where(keep, spread[rows:], 0.0).astype(BF16)

    shape = (level_ranks * pad, levels)
    r = iota(shape, 0)
    level = jnp.where(r % pad < levels_out, (r // pad) * levels_out + r % pad, -1)
    spread_levels = (iota(shape, 1) == level).astype(F32).astype(BF16)
    sums = []
    for f in range(fields):
        operator = dot(spread_levels, ops_ref[f]).astype(BF16)
        field = spectral_ref[:, f].reshape(cols, levels)
        vertical = dot(field, operator, NT).astype(BF16)
        sums.append(dot(basis, vertical))
        if f == 2:
            sums.insert(2, dot(slope_basis, vertical))

    south = jnp.where(rank * width < half, 1.0, -1.0)
    lane_field = iota((rows, FIELDS * pad), 1) // pad
    factor = jnp.where(lane_field == 2, -south, south)
    for d in range(level_ranks):
        joined = jnp.concatenate([x[:, d * pad : (d + 1) * pad] for x in sums], axis=1)
        mirrored = joined * factor
        for j in range(lats):
            piece = slice(j * parts * sub, (j + 1) * parts * sub)
            send_ref[j * level_ranks + d] = joined[piece].astype(BF16)
            send_ref[(lats + j) * level_ranks + d] = mirrored[piece].astype(BF16)


def modulo(values, modulus):
    quotient = jnp.floor(values / modulus)
    left = values - quotient * modulus
    left = jnp.where(left < 0, left + modulus, left)
    return jnp.where(left >= modulus, left - modulus, left)


def wave_column(pairs_ref, total_waves):
    slots = pairs_ref.shape[1]
    shape = (2 * slots, slots)
    mine = iota(shape, 1) == iota(shape, 0) // 2
    numbers = jnp.broadcast_to(pairs_ref[...], shape)
    number = jnp.sum(jnp.where(mine, numbers, 0).astype(F32), axis=1, keepdims=True)
    second = iota(number.shape, 0) % 2 == 1
    return jnp.where(second, total_waves - 1 - number, number)


def basis_kernel(total_waves, group, counts_ref, pairs_ref, basis_ref):
    count = counts_ref[lax.axis_index("wave")].astype(F32)
    waves = wave_column(pairs_ref, total_waves)
    weight = jnp.where(waves == 0, 1.0, jnp.where(2 * waves < count, 2.0, 0.0))
    tiles = NLON // LANES

    def table(step, length):
        turns = modulo(waves * (step * iota((1, length), 1)).astype(F32), count)
        angle = (2.0 * math.pi) * turns / count
        return jnp.cos(angle), jnp.sin(angle)

    coarse_cos, coarse_sin = table(LANES, LANES)
    fine_cos, fine_sin = table(1, LANES)
    coarse_cos, coarse_sin = coarse_cos * weight, coarse_sin * weight
    for t in range(tiles):
        a, b = coarse_cos[:, t : t + 1], coarse_sin[:, t : t + 1]
        cosine = (a * fine_cos - b * fine_sin).reshape(-1, 1, group, LANES)
        sine = (b * fine_cos + a * fine_sin).reshape(-1, 1, group, LANES)
        both = jnp.concatenate([cosine, -sine], axis=1).reshape(-1, LANES)
        basis_ref[:, t * LANES : (t + 1) * LANES] = both.astype(BF16)


def grid_kernel(sizes, counts_ref, sine_ref, pairs_ref, received_ref, basis_ref, out_ref):
    level_ranks, levels_out, pad, group, total_waves = sizes
    lats = sine_ref.shape[0]
    row = lax.axis_index("wave")
    count = counts_ref[row]
    sine = jnp.where(row < lats, sine_ref[lax.rem(row, lats)], -sine_ref[lax.rem(row, lats)])
    chunks, chunk_rows, lanes = received_ref.shape
    sources = chunks // level_ranks
    data = received_ref[...].astype(F32).reshape(sources, level_ranks, chunk_rows, lanes)
    total = jnp.sum(data, axis=1)

    waves = wave_column(pairs_ref, total_waves).reshape(sources, group, 1) / total_waves
    real, imag = total[:, :group], total[:, group:]
    turned = jnp.concatenate([-waves * imag, waves * real], axis=1)
    zonal_lane = iota(total.shape, 2) // pad == 3
    total = jnp.where(zonal_lane, turned, total).reshape(sources * chunk_rows, lanes)
    by_level = total.T
    keep = -(-levels_out // 8) * 8
    coeffs = jnp.concatenate([by_level[g * pad : g * pad + keep] for g in range(FIELDS)], axis=0)
    coeffs = coeffs.astype(BF16)

    inverse = 1.0 / (1.0 - jnp.full((1, 1), sine * sine))
    for start in range(0, NLON, COLS):
        values = dot(coeffs, basis_ref[:, start : start + COLS])
        first, second, third, fourth = (values[g * keep : g * keep + levels_out] for g in range(4))
        result = -(first * fourth * inverse + second * third * (1.0 / total_waves))
        inside = start + iota(result.shape, 1) < count
        out_ref[:, 0, start : start + COLS] = jnp.where(inside, result, 0.0)


def per_device(spectral, vertical_ops, legendre, legendre_slope, sine_lat, pair_map, lon_counts):
    pairs, _, parts, levels, width = spectral.shape
    level_ranks = lax.axis_size("lev")
    rows = lax.axis_size("wave")
    slots = pair_map.shape[0]
    total_waves = 2 * slots
    levels_out = levels // level_ranks
    pad = LANES // FIELDS
    lats = sine_lat.shape[0]
    orders = legendre.shape[1]
    group = pairs * orders
    assert rows == 2 * lats == lon_counts.shape[0]
    assert levels_out <= pad
    assert (width * level_ranks // 2) % width == 0

    smem = pl.BlockSpec(memory_space=pltpu.SMEM)
    vmem = pl.BlockSpec(memory_space=pltpu.VMEM)
    by_position = jnp.transpose(spectral, (0, 1, 2, 4, 3))
    pair_row = pair_map.reshape(1, slots)
    send = pl.pallas_call(
        functools.partial(partial_kernel, (pairs, level_ranks, levels_out, pad, total_waves)),
        out_shape=jax.ShapeDtypeStruct((rows * level_ranks, parts * group, FIELDS * pad), BF16),
        in_specs=[smem, vmem, vmem, vmem, vmem],
        out_specs=vmem,
        scratch_shapes=[pltpu.VMEM((2 * group * lats, legendre.shape[3]), F32)],
        name="partial_sums",
    )(pair_map, by_position, vertical_ops, legendre, legendre_slope)
    received = lax.all_to_all(send, ("wave", "lev"), split_axis=0, concat_axis=0, tiled=True)
    basis = pl.pallas_call(
        functools.partial(basis_kernel, total_waves, group),
        out_shape=jax.ShapeDtypeStruct((4 * slots, NLON), BF16),
        in_specs=[smem, vmem],
        out_specs=vmem,
        name="zonal_basis",
    )(lon_counts, pair_row)
    return pl.pallas_call(
        functools.partial(grid_kernel, (level_ranks, levels_out, pad, group, total_waves)),
        out_shape=jax.ShapeDtypeStruct((levels_out, 1, NLON), F32),
        in_specs=[smem, smem, vmem, vmem, vmem],
        out_specs=vmem,
        name="grid_tendency",
    )(lon_counts, sine_lat, pair_row, received, basis)


def solution(mesh):
    placed = (
        P("wave", None, None, None, "lev"),
        P(),
        P("wave", None, None, None),
        P("wave", None, None, None),
        P(),
        P(),
        P(),
    )
    return jax.shard_map(
        per_device, mesh=mesh, in_specs=placed, out_specs=P("lev", "wave", None), check_vma=False
    )
```

time: 65 us -> 22.3 us (0.34)
  other arithmetic: 24.4 us -> 0 us
  local copies, waits for them, and re-layouts: 16.5 us -> 0.67 us
  Pallas kernels: 0 us -> 8.67 us
  matrix products: 5.13 us -> 0 us
  between operations: 3.48 us -> 0.01 us
  starting transfers between devices: 10.6 us -> 7.33 us
  waiting for transfers between devices: 3.31 us -> 5.36 us
  loops' own time: 1.02 us -> 0 us
    pallas_call x0 -> x3, Pallas kernels: none -> 8.67 us  [the longest x1 3.09 us: per_device(): pl.pallas_call(functools.partial(partial_kernel, (pairs, level_ranks, lev...]
    cos x20 -> x0, other arithmetic: 7.99 us -> none  [angle_table(): return (jnp.cos(angles), jnp.sin(angles))]
    neg x21 -> x0, other arithmetic: 6.43 us -> none  [the longest x10 6.37 us: basis_block(): -weight[:, None] * sine_part]
    convert_element_type x12 -> x0, other arithmetic: 6.38 us -> none  [the longest x10 6.35 us: basis_block(): inside = (columns < lon_count).astype(jnp.float32)[None, :]]
    unnamed x18 -> x2, local copies, waits for them, and re-layouts: 6.62 us -> 0.67 us
    dot_general x25 -> x0, matrix products: 5.13 us -> none  [the longest x10 1.42 us: block_step(): jnp.dot(turning_coeffs, turning, preferred_element_type=jnp.float32)]
    all_to_all x2 -> x1, starting transfers between devices: 10.6 us -> 7.33 us  [per_device(): lax.all_to_all(send, ('wave', 'lev'), split_axis=0, concat_axis=0, tiled=...]
    add x21 -> x0, other arithmetic: 2.14 us -> none  [the longest x10 2.05 us: basis_block(): coarse_sin[:, :, None] * fine_cos[:, None, :]]
  transfers between devices with their start and end apart: 2 -> 1, of which waited for: 2 -> 1; matrix products, arithmetic and copies ran while one was open for 3% -> 0% of each run, Pallas kernels for 0% -> 13%
where the time goes in v1:
time: 22.3 us; the launch traced here: 22 us
  Pallas kernels  8.67 us (39%)
  starting transfers between devices  7.33 us (33%)
  waiting for transfers between devices  5.36 us (24%)
  local copies, waits for them, and re-layouts  0.67 us (3%)
    all_to_all x1, starting transfers between devices, per_device(): lax.all_to_all(send, ('wave', 'lev'), split_axis=0, concat_axis=0, tiled=...  7.33 us
    all_to_all x1, waiting for transfers between devices, per_device(): lax.all_to_all(send, ('wave', 'lev'), split_axis=0, concat_axis=0, tiled=...  5.36 us
    pallas_call x1, Pallas kernels, per_device(): pl.pallas_call(functools.partial(partial_kernel, (pairs, level_ranks, lev...  3.09 us
    pallas_call x1, Pallas kernels, per_device(): pl.pallas_call(functools.partial(basis_kernel, total_waves, group), out_s...  2.84 us
    pallas_call x1, Pallas kernels, per_device(): pl.pallas_call(functools.partial(grid_kernel, (level_ranks, levels_out, p...  2.74 us
    unnamed x2, local copies, waits for them, and re-layouts  0.67 us
  transfers between devices with their start and end apart: 1, of which 1 were waited for; matrix products, arithmetic and copies ran while one was open for 0% of the time, Pallas kernels for 13%

profile of v1, /device:TPU:0, one launch (start us, length us, event | category | flops | bytes accessed | tf_op | source)
XLA Modules:
  0.0 22.0 jit_solution(1136149613685951012)
XLA Ops:
  0.0 3.1 %partial_sums.1 = bf16[32,16,128]{2,1,0:T(8,128)(2,1)} custom-call(s32[32]{0:T(128)} %pair_ref.1, bf16[4,3,2,48,72]{4,3,2,1,0:T(8,128)(2,1)} %bitcast.2, bf16[3,72,72]{2,1,0:T(8,128)(2,1)} %ops_ref.1, bf16[4,2,4,192]{3,2,1,0:T(4,128)(2,1)} %legendre_ref.1, bf16[4,2,4,192]{3,2,1,0:T(4,128)(2,1)} %slope_ref.1), custom_call_target="tpu_custom_call" | custom-call | tf_op jit(solution)/shard_map/partial_sums/pallas_call | solution.py:198
  3.1 7.3 %all-to-all-start = ((bf16[32,16,128]{2,1,0:T(8,128)(2,1)}), bf16[32,16,128]{2,1,0:T(8,128)(2,1)S(1)}, u32[]{:S(2)}, u32[]{:S(2)}) async-start(bf16[32,16,128]{2,1,0:T(8,128)(2,1)} %partial_sums.1), calls=%async_computation | async-start | bytes 262144 | tf_op jit(solution)/shard_map/all_to_all | solution.py:206
  10.4 2.8 %zonal_basis.1.basis_ref = bf16[128,5120]{1,0:T(8,128)(2,1)} custom-call(s32[8]{0:T(128)} %counts_ref.3, s32[1,32]{1,0:T(1,128)} %bitcast.3), custom_call_target="tpu_custom_call" | custom-call | tf_op jit(solution)/shard_map/zonal_basis/pallas_call | solution.py:207
  13.3 5.4 %all-to-all-done.received_ref = bf16[32,16,128]{2,1,0:T(8,128)(2,1)S(1)} async-done(((bf16[32,16,128]{2,1,0:T(8,128)(2,1)}), bf16[32,16,128]{2,1,0:T(8,128)(2,1)S(1)}, u32[]{:S(2)}, u32[]{:S(2)}) %all-to-all-start) | async-done | bytes 131104 | tf_op jit(solution)/shard_map/all_to_all | solution.py:206
  18.6 0.0 copy-start
  18.6 0.7 %copy-done = bf16[32,16,128]{2,1,0:T(8,128)(2,1)} copy-done((bf16[32,16,128]{2,1,0:T(8,128)(2,1)}, bf16[32,16,128]{2,1,0:T(8,128)(2,1)S(1)}, u32[]{:S(2)}) %copy-start) | copy-done | bytes 131096
  19.3 2.7 %grid_tendency.1 = f32[18,1,5120]{2,1,0:T(1,128)} custom-call(s32[8]{0:T(128)} %counts_ref.3, f32[4]{0:T(128)} %sine_ref.1, s32[1,32]{1,0:T(1,128)} %bitcast.4, bf16[32,16,128]{2,1,0:T(8,128)(2,1)} %copy-done, bf16[128,5120]{1,0:T(8,128)(2,1)} %zonal_basis.1.basis_ref), custom_call_target="tpu_custom_call" | custom-call | tf_op jit(solution)/shard_map/grid_tendency/pallas_call | solution.py:214
Async XLA Ops:
  3.1 15.5 %all-to-all-start = ((bf16[32,16,128]{2,1,0:T(8,128)(2,1)}), bf16[32,16,128]{2,1,0:T(8,128)(2,1)S(1)}, u32[]{:S(2)}, u32[]{:S(2)}) async-start(bf16[32,16,128]{2,1,0:T(8,128)(2,1)} %partial_sums.1), calls=%async_computation | async-start | bytes 262144 | tf_op jit(solution)/shard_map/all_to_all | solution.py:206
  18.6 0.7 %copy-start = (bf16[32,16,128]{2,1,0:T(8,128)(2,1)}, bf16[32,16,128]{2,1,0:T(8,128)(2,1)S(1)}, u32[]{:S(2)}) copy-start(bf16[32,16,128]{2,1,0:T(8,128)(2,1)S(1)} %all-to-all-done.received_ref) | copy-start | bytes 393220

commit v2 on v1

--- a/solution.py
+++ b/solution.py
@@ -11,7 +11,8 @@
 NLON = 5120
 FIELDS = 4
 LANES = 128
-COLS = 512
+COLS = 1280
+RESIDENT = 4 << 20
 
 F32 = jnp.float32
 BF16 = jnp.bfloat16
@@ -36,11 +37,34 @@
 
 
 def partial_kernel(
-    sizes, pair_ref, spectral_ref, ops_ref, legendre_ref, slope_ref, send_ref, table_ref
+    sizes,
+    pair_hbm,
+    spectral_hbm,
+    ops_hbm,
+    legendre_hbm,
+    slope_hbm,
+    send_ref,
+    pair_ref,
+    spectral_ref,
+    ops_ref,
+    legendre_ref,
+    slope_ref,
+    table_ref,
+    arrived,
 ):
     pairs, level_ranks, levels_out, pad, total_waves = sizes
     _, fields, parts, width, levels = spectral_ref.shape
     _, orders, lats, full = legendre_ref.shape
+    copies = [
+        pltpu.make_async_copy(source, target, arrived.at[index])
+        for index, (source, target) in enumerate(
+            [(legendre_hbm, legendre_ref), (slope_hbm, slope_ref), (pair_hbm, pair_ref)]
+            + [(ops_hbm, ops_ref)]
+            + [(spectral_hbm.at[:, f], spectral_ref.at[:, f]) for f in range(fields)]
+        )
+    ]
+    for copy in copies:
+        copy.start()
     half = full // 2
     rank = lax.axis_index("lev")
     first_pair = lax.axis_index("wave") * pairs
@@ -48,6 +72,19 @@
     rows = lats * parts * sub
     cols = pairs * parts * width
 
+    r = iota((2 * rows, 2 * sub * lats), 0)
+    t, j, sw = r // rows, (r % rows) // (parts * sub), r % sub
+    wanted = (t * sub + sw) * lats + j
+    pick = (iota(r.shape, 1) == wanted).astype(F32).astype(BF16)
+    shape = (full, cols)
+    place = (iota(shape, 0) == rank * width + iota(shape, 1) % width).astype(F32).astype(BF16)
+    shape = (level_ranks * pad, levels)
+    r = iota(shape, 0)
+    level = jnp.where(r % pad < levels_out, (r // pad) * levels_out + r % pad, -1)
+    spread_levels = (iota(shape, 1) == level).astype(F32).astype(BF16)
+
+    for copy in copies[:2]:
+        copy.wait()
     for t, ref in enumerate((legendre_ref, slope_ref)):
         for s in range(pairs):
             for w in range(orders):
@@ -55,15 +92,10 @@
                 table_ref[base : base + lats, :] = ref[s, w].astype(F32)
     table = table_ref[...].astype(BF16)
 
-    r = iota((2 * rows, 2 * sub * lats), 0)
-    t, j, sw = r // rows, (r % rows) // (parts * sub), r % sub
-    wanted = (t * sub + sw) * lats + j
-    pick = (iota(r.shape, 1) == wanted).astype(F32).astype(BF16)
     picked = dot(pick, table).astype(BF16)
-    shape = (full, cols)
-    place = (iota(shape, 0) == rank * width + iota(shape, 1) % width).astype(F32).astype(BF16)
     spread = dot(picked, place)
 
+    copies[2].wait()
     shape = (rows, cols)
     r, col = iota(shape, 0), iota(shape, 1)
     part, slot, order = (r // sub) % parts, (r % sub) // orders, r % orders
@@ -82,12 +114,10 @@
     basis = jnp.where(keep, spread[:rows], 0.0).astype(BF16)
     slope_basis = jnp.where(keep, spread[rows:], 0.0).astype(BF16)
 
-    shape = (level_ranks * pad, levels)
-    r = iota(shape, 0)
-    level = jnp.where(r % pad < levels_out, (r // pad) * levels_out + r % pad, -1)
-    spread_levels = (iota(shape, 1) == level).astype(F32).astype(BF16)
     sums = []
+    copies[3].wait()
     for f in range(fields):
+        copies[4 + f].wait()
         operator = dot(spread_levels, ops_ref[f]).astype(BF16)
         field = spectral_ref[:, f].reshape(cols, levels)
         vertical = dot(field, operator, NT).astype(BF16)
@@ -124,9 +154,17 @@
     return jnp.where(second, total_waves - 1 - number, number)
 
 
-def basis_kernel(total_waves, group, counts_ref, pairs_ref, basis_ref):
-    count = counts_ref[lax.axis_index("wave")].astype(F32)
+def basis_kernel(total_waves, group, counts_ref, sine_ref, pairs_ref, basis_ref, aux_ref):
+    lats = sine_ref.shape[0]
+    row = lax.axis_index("wave")
+    count = counts_ref[row].astype(F32)
     waves = wave_column(pairs_ref, total_waves)
+    wave_rows = waves.shape[0]
+    sine = jnp.where(row < lats, sine_ref[lax.rem(row, lats)], -sine_ref[lax.rem(row, lats)])
+    inverse = 1.0 / (1.0 - jnp.full((8, LANES), sine * sine))
+    aux_ref[:wave_rows] = jnp.broadcast_to(waves / total_waves, (wave_rows, LANES))
+    aux_ref[wave_rows : wave_rows + 8] = inverse
+    aux_ref[wave_rows + 8 :] = jnp.full((8, LANES), count)
     weight = jnp.where(waves == 0, 1.0, jnp.where(2 * waves < count, 2.0, 0.0))
     tiles = NLON // LANES
 
@@ -146,18 +184,15 @@
         basis_ref[:, t * LANES : (t + 1) * LANES] = both.astype(BF16)
 
 
-def grid_kernel(sizes, counts_ref, sine_ref, pairs_ref, received_ref, basis_ref, out_ref):
+def grid_kernel(sizes, received_ref, basis_ref, aux_ref, out_hbm, out_ref, sent):
     level_ranks, levels_out, pad, group, total_waves = sizes
-    lats = sine_ref.shape[0]
-    row = lax.axis_index("wave")
-    count = counts_ref[row]
-    sine = jnp.where(row < lats, sine_ref[lax.rem(row, lats)], -sine_ref[lax.rem(row, lats)])
     chunks, chunk_rows, lanes = received_ref.shape
     sources = chunks // level_ranks
     data = received_ref[...].astype(F32).reshape(sources, level_ranks, chunk_rows, lanes)
     total = jnp.sum(data, axis=1)
 
-    waves = wave_column(pairs_ref, total_waves).reshape(sources, group, 1) / total_waves
+    wave_rows = sources * group
+    waves = aux_ref[:wave_rows].reshape(sources, group, LANES)
     real, imag = total[:, :group], total[:, group:]
     turned = jnp.concatenate([-waves * imag, waves * real], axis=1)
     zonal_lane = iota(total.shape, 2) // pad == 3
@@ -167,13 +202,23 @@
     coeffs = jnp.concatenate([by_level[g * pad : g * pad + keep] for g in range(FIELDS)], axis=0)
     coeffs = coeffs.astype(BF16)
 
-    inverse = 1.0 / (1.0 - jnp.full((1, 1), sine * sine))
+    inverse = aux_ref[wave_rows : wave_rows + 1, :1]
+    count = aux_ref[wave_rows + 8 : wave_rows + 9, :1]
+    copies = []
     for start in range(0, NLON, COLS):
         values = dot(coeffs, basis_ref[:, start : start + COLS])
         first, second, third, fourth = (values[g * keep : g * keep + levels_out] for g in range(4))
         result = -(first * fourth * inverse + second * third * (1.0 / total_waves))
-        inside = start + iota(result.shape, 1) < count
+        inside = (start + iota(result.shape, 1)).astype(F32) < count
+        window = (slice(None), slice(None), slice(start, start + COLS))
         out_ref[:, 0, start : start + COLS] = jnp.where(inside, result, 0.0)
+        copy = pltpu.make_async_copy(
+            out_ref.at[window], out_hbm.at[window], sent.at[start // COLS]
+        )
+        copy.start()
+        copies.append(copy)
+    for copy in copies:
+        copy.wait()
 
 
 def per_device(spectral, vertical_ops, legendre, legendre_slope, sine_lat, pair_map, lon_counts):
@@ -193,31 +238,54 @@
 
     smem = pl.BlockSpec(memory_space=pltpu.SMEM)
     vmem = pl.BlockSpec(memory_space=pltpu.VMEM)
+    hbm = pl.BlockSpec(memory_space=pl.ANY)
     by_position = jnp.transpose(spectral, (0, 1, 2, 4, 3))
-    pair_row = pair_map.reshape(1, slots)
+    fields = spectral.shape[1]
+    resident = 4 * slots * NLON * 2 <= RESIDENT
+    placed = pltpu.VMEM if resident else jax.ShapeDtypeStruct
     send = pl.pallas_call(
         functools.partial(partial_kernel, (pairs, level_ranks, levels_out, pad, total_waves)),
-        out_shape=jax.ShapeDtypeStruct((rows * level_ranks, parts * group, FIELDS * pad), BF16),
-        in_specs=[smem, vmem, vmem, vmem, vmem],
+        out_shape=pltpu.VMEM((rows * level_ranks, parts * group, FIELDS * pad), BF16),
+        in_specs=[hbm] * 5,
         out_specs=vmem,
-        scratch_shapes=[pltpu.VMEM((2 * group * lats, legendre.shape[3]), F32)],
+        scratch_shapes=[
+            pltpu.SMEM(pair_map.shape, pair_map.dtype),
+            pltpu.VMEM(by_position.shape, BF16),
+            pltpu.VMEM(vertical_ops.shape, BF16),
+            pltpu.VMEM(legendre.shape, BF16),
+            pltpu.VMEM(legendre.shape, BF16),
+            pltpu.VMEM((2 * group * lats, legendre.shape[3]), F32),
+            pltpu.SemaphoreType.DMA((4 + fields,)),
+        ],
         name="partial_sums",
     )(pair_map, by_position, vertical_ops, legendre, legendre_slope)
     received = lax.all_to_all(send, ("wave", "lev"), split_axis=0, concat_axis=0, tiled=True)
-    basis = pl.pallas_call(
+    basis, aux = pl.pallas_call(
         functools.partial(basis_kernel, total_waves, group),
-        out_shape=jax.ShapeDtypeStruct((4 * slots, NLON), BF16),
-        in_specs=[smem, vmem],
-        out_specs=vmem,
+        out_shape=[
+            placed((4 * slots, NLON), BF16),
+            pltpu.VMEM((2 * slots + 16, LANES), F32),
+        ],
+        in_specs=[smem, smem, vmem],
+        out_specs=[vmem, vmem],
         name="zonal_basis",
-    )(lon_counts, pair_row)
+    )(lon_counts, sine_lat, pair_map.reshape(1, slots))
+    received, aux = (
+        pltpu.with_memory_space_constraint(x, pltpu.VMEM) for x in (received, aux)
+    )
+    if resident:
+        basis = pltpu.with_memory_space_constraint(basis, pltpu.VMEM)
     return pl.pallas_call(
         functools.partial(grid_kernel, (level_ranks, levels_out, pad, group, total_waves)),
         out_shape=jax.ShapeDtypeStruct((levels_out, 1, NLON), F32),
-        in_specs=[smem, smem, vmem, vmem, vmem],
-        out_specs=vmem,
+        in_specs=[vmem, vmem, vmem],
+        out_specs=hbm,
+        scratch_shapes=[
+            pltpu.VMEM((levels_out, 1, NLON), F32),
+            pltpu.SemaphoreType.DMA((NLON // COLS,)),
+        ],
         name="grid_tendency",
-    )(lon_counts, sine_lat, pair_row, received, basis)
+    )(received, basis, aux)
 
 
 def solution(mesh):

time: 22.3 us -> 20.3 us (0.910)
  Pallas kernels: 8.67 us -> 6.3 us
  waiting for transfers between devices: 5.36 us -> 6.41 us
  local copies, waits for them, and re-layouts: 0.67 us -> 0 us
    pallas_call x1, Pallas kernels: 2.74 us -> 1.19 us  [per_device(): pl.pallas_call(functools.partial(grid_kernel, (level_ranks, levels_out, p...]
    pallas_call x1, Pallas kernels: 2.84 us -> 1.79 us  [per_device(): pl.pallas_call(functools.partial(basis_kernel, total_waves, group), out_s...]
    all_to_all x1, waiting for transfers between devices: 5.36 us -> 6.41 us  [per_device(): lax.all_to_all(send, ('wave', 'lev'), split_axis=0, concat_axis=0, tiled=...]
    unnamed x2 -> x0, local copies, waits for them, and re-layouts: 0.67 us -> none
    pallas_call x1, Pallas kernels: 3.09 us -> 3.32 us  [per_device(): pl.pallas_call(functools.partial(partial_kernel, (pairs, level_ranks, lev...]
  transfers between devices with their start and end apart: 1 -> 1, of which waited for: 1 -> 1; matrix products, arithmetic and copies ran while one was open for 0% -> 0% of each run, Pallas kernels for 13% -> 9%
where the time goes in v2:
time: 20.3 us; the launch traced here: 20.1 us
  starting transfers between devices  7.33 us (36%)
  waiting for transfers between devices  6.41 us (32%)
  Pallas kernels  6.3 us (31%)
    all_to_all x1, starting transfers between devices, per_device(): lax.all_to_all(send, ('wave', 'lev'), split_axis=0, concat_axis=0, tiled=...  7.33 us
    all_to_all x1, waiting for transfers between devices, per_device(): lax.all_to_all(send, ('wave', 'lev'), split_axis=0, concat_axis=0, tiled=...  6.41 us
    pallas_call x1, Pallas kernels, per_device(): pl.pallas_call(functools.partial(partial_kernel, (pairs, level_ranks, lev...  3.32 us
    pallas_call x1, Pallas kernels, per_device(): pl.pallas_call(functools.partial(basis_kernel, total_waves, group), out_s...  1.79 us
    pallas_call x1, Pallas kernels, per_device(): pl.pallas_call(functools.partial(grid_kernel, (level_ranks, levels_out, p...  1.19 us
  transfers between devices with their start and end apart: 1, of which 1 were waited for; matrix products, arithmetic and copies ran while one was open for 0% of the time, Pallas kernels for 9%

profile of v2, /device:TPU:0, one launch (start us, length us, event | category | flops | bytes accessed | tf_op | source)
XLA Modules:
  0.0 20.1 jit_solution(7833079850284183777)
XLA Ops:
  0.0 3.3 %partial_sums.1 = bf16[32,16,128]{2,1,0:T(8,128)(2,1)} custom-call(s32[32]{0:T(128)} %pair_hbm.1, bf16[4,3,2,48,72]{4,3,2,1,0:T(8,128)(2,1)} %bitcast.2, bf16[3,72,72]{2,1,0:T(8,128)(2,1)} %ops_hbm.1, bf16[4,2,4,192]{3,2,1,0:T(4,128)(2,1)} %legendre_hbm.1, bf16[4,2,4,192]{3,2,1,0:T(4,128)(2,1)} %slope_hbm.1), custom_call_target="tpu_custom_call" | custom-call | tf_op jit(solution)/shard_map/partial_sums/pallas_call | solution.py:246
  3.3 7.3 %all-to-all-start = ((bf16[32,16,128]{2,1,0:T(8,128)(2,1)}), bf16[32,16,128]{2,1,0:T(8,128)(2,1)S(1)}, u32[]{:S(2)}, u32[]{:S(2)}) async-start(bf16[32,16,128]{2,1,0:T(8,128)(2,1)} %partial_sums.1), calls=%async_computation | async-start | bytes 262144 | tf_op jit(solution)/shard_map/all_to_all | solution.py:262
  10.7 1.8 %zonal_basis.1 = (bf16[128,5120]{1,0:T(8,128)(2,1)S(1)}, f32[80,128]{1,0:T(8,128)S(1)}) custom-call(s32[8]{0:T(128)} %counts_ref.1, f32[4]{0:T(128)} %sine_ref.1, s32[1,32]{1,0:T(1,128)} %bitcast.3), custom_call_target="tpu_custom_call" | custom-call | tf_op jit(solution)/shard_map/zonal_basis/pallas_call | solution.py:263
  12.5 6.4 %all-to-all-done.received_ref = bf16[32,16,128]{2,1,0:T(8,128)(2,1)S(1)} async-done(((bf16[32,16,128]{2,1,0:T(8,128)(2,1)}), bf16[32,16,128]{2,1,0:T(8,128)(2,1)S(1)}, u32[]{:S(2)}, u32[]{:S(2)}) %all-to-all-start) | async-done | bytes 131104 | tf_op jit(solution)/shard_map/all_to_all | solution.py:262
  18.9 1.2 %grid_tendency.1 = f32[18,1,5120]{2,1,0:T(1,128)} custom-call(bf16[32,16,128]{2,1,0:T(8,128)(2,1)S(1)} %all-to-all-done.received_ref, bf16[128,5120]{1,0:T(8,128)(2,1)S(1)} %get-tuple-element.7.basis_ref, f32[80,128]{1,0:T(8,128)S(1)} %get-tuple-element.8.aux_ref), custom_call_target="tpu_custom_call" | custom-call | tf_op jit(solution)/shard_map/grid_tendency/pallas_call | solution.py:278
Async XLA Ops:
  3.3 15.5 %all-to-all-start = ((bf16[32,16,128]{2,1,0:T(8,128)(2,1)}), bf16[32,16,128]{2,1,0:T(8,128)(2,1)S(1)}, u32[]{:S(2)}, u32[]{:S(2)}) async-start(bf16[32,16,128]{2,1,0:T(8,128)(2,1)} %partial_sums.1), calls=%async_computation | async-start | bytes 262144 | tf_op jit(solution)/shard_map/all_to_all | solution.py:262

commit v3 on v2

v3 whole, which is shorter than its diff:
```python
import functools
import math

import jax
import jax.numpy as jnp
from jax import lax
from jax.experimental import pallas as pl
from jax.experimental.pallas import tpu as pltpu
from jax.sharding import PartitionSpec as P

NLON = 5120
FIELDS = 4
LANES = 128
COLS = 1280
RESIDENT = 4 << 20

F32 = jnp.float32
BF16 = jnp.bfloat16
NT = (((1,), (1,)), ((), ()))


def dot(a, b, dims=(((1,), (0,)), ((), ()))):
    return lax.dot_general(a, b, dims, preferred_element_type=F32)


def iota(shape, dim):
    return lax.broadcasted_iota(jnp.int32, shape, dim)


def cos_sin(products, count, inverse):
    quarters = jnp.floor(products * 4.0 * inverse + 0.5)
    angle = (products * 4.0 - quarters * count) * inverse * (0.5 * math.pi)
    square = angle * angle
    sine = square * (1.0 / 362880.0) - 1.0 / 5040.0
    sine = square * sine + 1.0 / 120.0
    sine = square * sine - 1.0 / 6.0
    sine = angle + angle * (square * sine)
    cosine = square * (1.0 / 40320.0) - 1.0 / 720.0
    cosine = square * cosine + 1.0 / 24.0
    cosine = square * cosine - 0.5
    cosine = square * cosine + 1.0
    turn = quarters.astype(jnp.int32) & 3
    swap = (turn & 1) == 1
    first = jnp.where(swap, sine, cosine)
    second = jnp.where(swap, cosine, sine)
    first = jnp.where((turn == 1) | (turn == 2), -first, first)
    second = jnp.where(turn >= 2, -second, second)
    return first, second


def zonal_tables(sizes, count, sine, pair_ref, basis_ref, aux_ref, coarse_ref):
    pairs, orders, parts, total_waves = sizes
    lanes = basis_ref.shape[1]
    sub = pairs * orders
    shape = (8, lanes)
    lane = iota(shape, 1)
    slot = (lane // (parts * sub)) * pairs + (lane % sub) // orders
    number = jnp.zeros(shape, jnp.int32)
    for index in range(total_waves // 2):
        number = jnp.where(slot == index, pair_ref[index], number)
    waves = jnp.where(lane % orders == 1, total_waves - 1 - number, number).astype(F32)
    imag = (lane // sub) % parts == 1
    aux_ref[:8] = jnp.where(imag, waves, -waves) / total_waves
    aux_ref[8:16] = 1.0 / (1.0 - jnp.full(shape, sine * sine))
    aux_ref[16:] = jnp.full(shape, count)
    weight = jnp.where(waves == 0, 1.0, jnp.where(2 * waves < count, 2.0, 0.0))[:1]
    inverse = 1.0 / jnp.full(shape, count)[:1]
    waves, imag = waves[:1], imag[:1]
    tiles = NLON // LANES
    coarse_cos, coarse_sin = cos_sin(
        waves * (LANES * iota((tiles, lanes), 0)).astype(F32), count, inverse
    )
    fine_cos, fine_sin = cos_sin(waves * iota((LANES, lanes), 0).astype(F32), count, inverse)
    coarse_ref[0], coarse_ref[1] = coarse_cos * weight, coarse_sin * weight
    first = jnp.where(imag, -fine_sin, fine_cos)
    second = jnp.where(imag, -fine_cos, -fine_sin)
    for t in range(tiles):
        a, b = coarse_ref[0, t : t + 1], coarse_ref[1, t : t + 1]
        basis_ref[t * LANES : (t + 1) * LANES] = (a * first + b * second).astype(BF16)


def front_kernel(
    sizes,
    counts_hbm,
    sine_hbm,
    pair_hbm,
    legendre_hbm,
    slope_hbm,
    ops_hbm,
    spectral_hbm,
    send_ref,
    basis_ref,
    aux_ref,
    counts_ref,
    sine_ref,
    pair_ref,
    legendre_ref,
    slope_ref,
    ops_ref,
    spectral_ref,
    table_ref,
    joined_ref,
    coarse_ref,
    arrived,
):
    level_ranks, levels_out, pad, total_waves = sizes
    pairs, fields, parts, width, levels = spectral_ref.shape
    _, orders, lats, full = legendre_ref.shape
    half = full // 2
    rank, row = lax.axis_index("lev"), lax.axis_index("wave")
    first_pair = row * pairs
    sub = pairs * orders
    rows = orders * lats
    copies = [
        pltpu.make_async_copy(source, target, arrived.at[index])
        for index, (source, target) in enumerate(
            [
                (counts_hbm, counts_ref),
                (sine_hbm, sine_ref),
                (pair_hbm, pair_ref),
                (legendre_hbm, legendre_ref),
                (slope_hbm, slope_ref),
                (ops_hbm, ops_ref),
            ]
            + [(spectral_hbm.at[:, f], spectral_ref.at[:, f]) for f in range(fields)]
        )
    ]
    for copy in copies:
        copy.start()

    for copy in copies[:3]:
        copy.wait()
    north = lax.rem(row, lats)
    sine = jnp.where(row < lats, sine_ref[north], -sine_ref[north])
    count = counts_ref[row].astype(F32)
    zonal = (pairs, orders, parts, total_waves)
    zonal_tables(zonal, count, sine, pair_ref, basis_ref, aux_ref, coarse_ref)

    for copy in copies[3:]:
        copy.wait()
    for t, ref in enumerate((legendre_ref, slope_ref)):
        for s in range(pairs):
            for w in range(orders):
                base = ((t * pairs + s) * orders + w) * lats
                table_ref[base : base + lats, :] = ref[s, w].astype(F32)
    table = table_ref[...]
    piece = table[:, :width]
    for b in range(1, level_ranks):
        piece = jnp.where(rank == b, table[:, b * width : (b + 1) * width], piece)
    shape = piece.shape
    r, position = iota(shape, 0), rank * width + iota(shape, 1)
    slot, order = (r // rows) % pairs, (r // lats) % orders
    number = jnp.zeros(shape, jnp.int32)
    for s in range(pairs):
        number = jnp.where(slot == s, pair_ref[first_pair + s], number)
    upper = (position >= half).astype(jnp.int32)
    offset = position - half * upper
    count0 = (total_waves - number + 1 - upper) >> 1
    count1 = (number + 2 - upper) >> 1
    low = jnp.where(order == 0, 0, count0)
    high = jnp.where(order == 0, count0, count0 + count1)
    piece = jnp.where((offset >= low) & (offset < high), piece, 0.0)
    plain = [piece[s * rows : (s + 1) * rows] for s in range(pairs)]
    slope = [piece[(pairs + s) * rows : (pairs + s + 1) * rows] for s in range(pairs)]
    both = [jnp.concatenate([a, b], axis=0).astype(BF16) for a, b in zip(plain, slope)]
    plain = [a.astype(BF16) for a in plain]

    sums = [[] for _ in range(FIELDS)]
    for f in range(fields):
        field = spectral_ref[:, f].reshape(pairs * parts * width, levels)
        vertical = dot(field, ops_ref[f], NT).astype(BF16)
        for c in range(parts):
            for s in range(pairs):
                start = (s * parts + c) * width
                block = vertical[start : start + width]
                if f == 2:
                    result = dot(both[s], block)
                    sums[2].append(result[rows:])
                    sums[3].append(result[:rows])
                else:
                    sums[f].append(dot(plain[s], block))

    sums = [jnp.concatenate(x, axis=0) for x in sums]
    sums = [jnp.pad(x, ((0, 0), (0, LANES - levels))) for x in sums]
    sums = [pltpu.roll(x, g * pad, 1) if g else x for g, x in enumerate(sums)]
    lane = iota(sums[0].shape, 1)
    south = jnp.where(rank * width < half, 1.0, -1.0)
    piece_rows = parts * sub
    factor = jnp.where(iota((piece_rows, LANES), 1) // pad == 2, -south, south)
    for d in range(level_ranks):
        shift = d * levels_out
        lane_field = ((lane + (LANES - shift)) % LANES) // pad
        joined = sums[FIELDS - 1]
        for g in range(FIELDS - 1):
            joined = jnp.where(lane_field == g, sums[g], joined)
        if shift:
            joined = pltpu.roll(joined, LANES - shift, 1)
        joined_ref[d] = joined
        for j in range(lats):
            own = joined_ref[d, pl.ds(j, piece_rows, stride=lats), :]
            send_ref[j * level_ranks + d] = own.astype(BF16)
            send_ref[(lats + j) * level_ranks + d] = (own * factor).astype(BF16)


def grid_kernel(sizes, received_ref, basis_ref, aux_ref, out_hbm, out_ref, sent):
    level_ranks, levels_out, pad, group, total_waves = sizes
    chunks, chunk_rows, lanes = received_ref.shape
    sources = chunks // level_ranks
    data = received_ref[...].astype(F32).reshape(sources, level_ranks, chunk_rows, lanes)
    total = jnp.sum(data, axis=1)

    by_level = total.reshape(sources * chunk_rows, lanes).T
    keep = -(-levels_out // 8) * 8
    coeffs = [by_level[g * pad : g * pad + keep] for g in range(FIELDS)]
    zonal = coeffs[3]
    span = zonal.shape[1]
    imag = (iota(zonal.shape, 1) // group) % 2 == 1
    swapped = jnp.where(imag, pltpu.roll(zonal, group, 1), pltpu.roll(zonal, span - group, 1))
    coeffs[3] = swapped * aux_ref[:1]
    coeffs = jnp.concatenate(coeffs, axis=0).astype(BF16)

    inverse, count = aux_ref[8:9, :1], aux_ref[16:17, :1]
    copies = []
    for start in range(0, NLON, COLS):
        values = dot(coeffs, basis_ref[start : start + COLS], NT)
        first, second, third, fourth = (values[g * keep : g * keep + levels_out] for g in range(4))
        result = -(first * fourth * inverse + second * third * (1.0 / total_waves))
        inside = (start + iota(result.shape, 1)).astype(F32) < count
        window = (slice(None), slice(None), slice(start, start + COLS))
        out_ref[:, 0, start : start + COLS] = jnp.where(inside, result, 0.0)
        copy = pltpu.make_async_copy(
            out_ref.at[window], out_hbm.at[window], sent.at[start // COLS]
        )
        copy.start()
        copies.append(copy)
    for copy in copies:
        copy.wait()


def per_device(spectral, vertical_ops, legendre, legendre_slope, sine_lat, pair_map, lon_counts):
    pairs, fields, parts, levels, width = spectral.shape
    level_ranks = lax.axis_size("lev")
    rows = lax.axis_size("wave")
    slots = pair_map.shape[0]
    total_waves = 2 * slots
    levels_out = levels // level_ranks
    pad = LANES // FIELDS
    lats, full = legendre.shape[2:]
    orders = legendre.shape[1]
    group = pairs * orders
    assert rows == 2 * lats == lon_counts.shape[0]
    assert levels_out <= pad and levels <= LANES
    assert (full // 2) % width == 0

    vmem = pl.BlockSpec(memory_space=pltpu.VMEM)
    hbm = pl.BlockSpec(memory_space=pl.ANY)
    by_position = jnp.transpose(spectral, (0, 1, 2, 4, 3))
    resident = 4 * slots * NLON * 2 <= RESIDENT
    placed = pltpu.VMEM if resident else jax.ShapeDtypeStruct
    sources = [lon_counts, sine_lat, pair_map]
    sources += [legendre, legendre_slope, vertical_ops, by_position]
    spaces = [pltpu.SMEM] * 3 + [pltpu.VMEM] * 4
    send, basis, aux = pl.pallas_call(
        functools.partial(front_kernel, (level_ranks, levels_out, pad, total_waves)),
        out_shape=[
            pltpu.VMEM((rows * level_ranks, parts * group, LANES), BF16),
            placed((NLON, 2 * parts * slots), BF16),
            pltpu.VMEM((24, 2 * parts * slots), F32),
        ],
        in_specs=[hbm] * len(sources),
        out_specs=[vmem] * 3,
        scratch_shapes=[space(x.shape, x.dtype) for space, x in zip(spaces, sources)]
        + [
            pltpu.VMEM((2 * group * lats, full), F32),
            pltpu.VMEM((level_ranks, parts * group * lats, LANES), F32),
            pltpu.VMEM((2, NLON // LANES, 2 * parts * slots), F32),
            pltpu.SemaphoreType.DMA((len(sources) - 1 + fields,)),
        ],
        name="front",
    )(*sources)
    received = lax.all_to_all(send, ("wave", "lev"), split_axis=0, concat_axis=0, tiled=True)
    received, aux = (
        pltpu.with_memory_space_constraint(x, pltpu.VMEM) for x in (received, aux)
    )
    if resident:
        basis = pltpu.with_memory_space_constraint(basis, pltpu.VMEM)
    return pl.pallas_call(
        functools.partial(grid_kernel, (level_ranks, levels_out, pad, group, total_waves)),
        out_shape=jax.ShapeDtypeStruct((levels_out, 1, NLON), F32),
        in_specs=[vmem, vmem, vmem],
        out_specs=hbm,
        scratch_shapes=[
            pltpu.VMEM((levels_out, 1, NLON), F32),
            pltpu.SemaphoreType.DMA((NLON // COLS,)),
        ],
        name="grid_tendency",
    )(received, basis, aux)


def solution(mesh):
    placed = (
        P("wave", None, None, None, "lev"),
        P(),
        P("wave", None, None, None),
        P("wave", None, None, None),
        P(),
        P(),
        P(),
    )
    return jax.shard_map(
        per_device, mesh=mesh, in_specs=placed, out_specs=P("lev", "wave", None), check_vma=False
    )
```

time: 20.3 us -> 18.9 us (0.931)
  blocking collectives: 0 us -> 15.3 us
  starting transfers between devices: 7.33 us -> 0 us
  waiting for transfers between devices: 6.41 us -> 0 us
  Pallas kernels: 6.3 us -> 3.38 us
    all_to_all x0 -> x1, blocking collectives: none -> 15.3 us  [per_device(): lax.all_to_all(send, ('wave', 'lev'), split_axis=0, concat_axis=0, tiled=...]
    all_to_all x1 -> x0, starting transfers between devices: 7.33 us -> none  [per_device(): lax.all_to_all(send, ('wave', 'lev'), split_axis=0, concat_axis=0, tiled=...]
    all_to_all x1 -> x0, waiting for transfers between devices: 6.41 us -> none  [per_device(): lax.all_to_all(send, ('wave', 'lev'), split_axis=0, concat_axis=0, tiled=...]
    pallas_call x2 -> x1, Pallas kernels: 5.11 us -> 2 us  [per_device(): pl.pallas_call(functools.partial(front_kernel, (level_ranks, levels_out,...]
  transfers between devices with their start and end apart: 1 -> 0, of which waited for: 1 -> 0; matrix products, arithmetic and copies ran while one was open for 0% -> 0% of each run, Pallas kernels for 9% -> 0%
where the time goes in v3:
time: 18.9 us; the launch traced here: 18.7 us
  blocking collectives  15.3 us (81%)
  Pallas kernels  3.38 us (18%)
    all_to_all x1, blocking collectives, per_device(): lax.all_to_all(send, ('wave', 'lev'), split_axis=0, concat_axis=0, tiled=...  15.3 us
    pallas_call x1, Pallas kernels, per_device(): pl.pallas_call(functools.partial(front_kernel, (level_ranks, levels_out,...  2 us
    pallas_call x1, Pallas kernels, per_device(): pl.pallas_call(functools.partial(grid_kernel, (level_ranks, levels_out, p...  1.38 us

profile of v3, /device:TPU:0, one launch (start us, length us, event | category | flops | bytes accessed | tf_op | source)
XLA Modules:
  0.0 18.7 jit_solution(10902996915004062355)
XLA Ops:
  0.0 2.0 %front.1 = (bf16[32,16,128]{2,1,0:T(8,128)(2,1)S(1)}, bf16[5120,128]{1,0:T(8,128)(2,1)S(1)}, f32[24,128]{1,0:T(8,128)S(1)}) custom-call(s32[8]{0:T(128)} %counts_hbm.1, f32[4]{0:T(128)} %sine_hbm.1, s32[32]{0:T(128)} %pair_hbm.1, bf16[4,2,4,192]{3,2,1,0:T(4,128)(2,1)} %legendre_hbm.1, bf16[4,2,4,192]{3,2,1,0:T(4,128)(2,1)} %slope_hbm.1, ...), custom_call_target="tpu_custom_call" | custom-call | tf_op jit(solution)/shard_map/front/pallas_call | solution.py:263
  2.0 15.3 %all_to_all.5.received_ref = bf16[32,16,128]{2,1,0:T(8,128)(2,1)S(1)} all-to-all(bf16[32,16,128]{2,1,0:T(8,128)(2,1)S(1)} %get-tuple-element.8), channel_id=1, replica_groups=mesh['wave'=8,'lev'=4] {'wave','lev'}, dimensions={0} | all-to-all | bytes 262144 | tf_op jit(solution)/shard_map/all_to_all | solution.py:281
  17.3 1.4 %grid_tendency.1 = f32[18,1,5120]{2,1,0:T(1,128)} custom-call(bf16[32,16,128]{2,1,0:T(8,128)(2,1)S(1)} %all_to_all.5.received_ref, bf16[5120,128]{1,0:T(8,128)(2,1)S(1)} %get-tuple-element.9.basis_ref, f32[24,128]{1,0:T(8,128)S(1)} %get-tuple-element.10.aux_ref), custom_call_target="tpu_custom_call" | custom-call | tf_op jit(solution)/shard_map/grid_tendency/pallas_call | solution.py:287

commit v4 on v3

--- a/solution.py
+++ b/solution.py
@@ -10,9 +10,11 @@
 
 NLON = 5120
 FIELDS = 4
+FIELD_OF = (0, 1, 2, 2)
 LANES = 128
-COLS = 1280
+COLUMNS = (1280, 1280, 1280, 768, 512)
 RESIDENT = 4 << 20
+RUN = NLON // LANES // 4
 
 F32 = jnp.float32
 BF16 = jnp.bfloat16
@@ -27,7 +29,7 @@
     return lax.broadcasted_iota(jnp.int32, shape, dim)
 
 
-def cos_sin(products, count, inverse):
+def cos_sin(products, count, inverse, quarter=0):
     quarters = jnp.floor(products * 4.0 * inverse + 0.5)
     angle = (products * 4.0 - quarters * count) * inverse * (0.5 * math.pi)
     square = angle * angle
@@ -39,7 +41,7 @@
     cosine = square * cosine + 1.0 / 24.0
     cosine = square * cosine - 0.5
     cosine = square * cosine + 1.0
-    turn = quarters.astype(jnp.int32) & 3
+    turn = (quarters.astype(jnp.int32) + quarter) & 3
     swap = (turn & 1) == 1
     first = jnp.where(swap, sine, cosine)
     second = jnp.where(swap, cosine, sine)
@@ -48,35 +50,74 @@
     return first, second
 
 
-def zonal_tables(sizes, count, sine, pair_ref, basis_ref, aux_ref, coarse_ref):
+def zonal_rows(sizes, count, sine, pair_ref, aux_ref):
     pairs, orders, parts, total_waves = sizes
-    lanes = basis_ref.shape[1]
     sub = pairs * orders
-    shape = (8, lanes)
+    shape = (8, aux_ref.shape[1])
     lane = iota(shape, 1)
     slot = (lane // (parts * sub)) * pairs + (lane % sub) // orders
     number = jnp.zeros(shape, jnp.int32)
     for index in range(total_waves // 2):
         number = jnp.where(slot == index, pair_ref[index], number)
     waves = jnp.where(lane % orders == 1, total_waves - 1 - number, number).astype(F32)
-    imag = (lane // sub) % parts == 1
-    aux_ref[:8] = jnp.where(imag, waves, -waves) / total_waves
-    aux_ref[8:16] = 1.0 / (1.0 - jnp.full(shape, sine * sine))
+    imag = (lane // sub) % parts
+    scale = 1.0 / (1.0 - jnp.full(shape, sine * sine)) / total_waves
+    aux_ref[:8] = waves
+    aux_ref[8:16] = jnp.where(imag == 1, -waves, waves) * scale
     aux_ref[16:] = jnp.full(shape, count)
-    weight = jnp.where(waves == 0, 1.0, jnp.where(2 * waves < count, 2.0, 0.0))[:1]
-    inverse = 1.0 / jnp.full(shape, count)[:1]
-    waves, imag = waves[:1], imag[:1]
-    tiles = NLON // LANES
-    coarse_cos, coarse_sin = cos_sin(
-        waves * (LANES * iota((tiles, lanes), 0)).astype(F32), count, inverse
-    )
-    fine_cos, fine_sin = cos_sin(waves * iota((LANES, lanes), 0).astype(F32), count, inverse)
-    coarse_ref[0], coarse_ref[1] = coarse_cos * weight, coarse_sin * weight
-    first = jnp.where(imag, -fine_sin, fine_cos)
-    second = jnp.where(imag, -fine_cos, -fine_sin)
-    for t in range(tiles):
-        a, b = coarse_ref[0, t : t + 1], coarse_ref[1, t : t + 1]
-        basis_ref[t * LANES : (t + 1) * LANES] = (a * first + b * second).astype(BF16)
+
+
+def zonal_table(group, aux_ref, rows_ref, fine_ref, basis_ref):
+    waves, count = aux_ref[:8], aux_ref[16:]
+    shape = waves.shape
+    lanes = shape[1]
+    weight = jnp.where(waves == 0, 1.0, jnp.where(2 * waves < count, 2.0, 0.0))
+    inverse = 1.0 / count
+    index = iota(shape, 0)
+    tile = (index // 2) * RUN + index % 2
+    cosine, sine_part = cos_sin(waves * (tile * LANES).astype(F32), count, inverse)
+    rows_ref[0], rows_ref[1] = cosine * weight, sine_part * weight
+    rows_ref[2] = 2.0 * cosine
+    groups = LANES // 8
+    index = iota((groups, lanes), 0)
+    cosine, sine_part = cos_sin(waves[:1] * (8 * index).astype(F32), count[:1], inverse[:1])
+    rows_ref[3 : 3 + groups // 8] = cosine.reshape(groups // 8, 8, lanes)
+    rows_ref[3 + groups // 8 :] = sine_part.reshape(groups // 8, 8, lanes)
+    imag = (iota(shape, 1) // group) % 2
+    lower_cos, lower_sin = cos_sin(waves * iota(shape, 0).astype(F32), count, inverse, imag)
+    for g in range(groups):
+        upper = pl.ds(g % 8, 1)
+        c, s = rows_ref[3 + g // 8, upper], rows_ref[3 + groups // 8 + g // 8, upper]
+        fine_ref[0, 8 * g : 8 * g + 8] = c * lower_cos - s * lower_sin
+        fine_ref[1, 8 * g : 8 * g + 8] = -(s * lower_cos + c * lower_sin)
+    def one(run, carry):
+        zonal_run(run, rows_ref, fine_ref, basis_ref)
+        return carry
+
+    lax.fori_loop(0, NLON // LANES // RUN, one, 0)
+
+
+def zonal_run(run, rows_ref, fine_ref, basis_ref):
+    twice = rows_ref[2, 1:2]
+
+    def first(t):
+        a, b = rows_ref[0, pl.ds(2 * run + t, 1)], rows_ref[1, pl.ds(2 * run + t, 1)]
+        return a * fine_ref[0] + b * fine_ref[1]
+
+    def store(t, tile):
+        start = pl.multiple_of((run * RUN + t) * LANES, LANES)
+        basis_ref[pl.ds(start, LANES)] = tile.astype(BF16)
+
+    before, here = first(0), first(1)
+    store(0, before)
+    store(1, here)
+    for t in range(2, RUN):
+        before, here = here, twice * here - before
+        store(t, here)
+
+
+def table_early():
+    return 2 * lax.axis_index("wave") < lax.axis_size("wave")
 
 
 def front_kernel(
@@ -100,7 +141,8 @@
     spectral_ref,
     table_ref,
     joined_ref,
-    coarse_ref,
+    rows_ref,
+    fine_ref,
     arrived,
 ):
     level_ranks, levels_out, pad, total_waves = sizes
@@ -134,9 +176,9 @@
     sine = jnp.where(row < lats, sine_ref[north], -sine_ref[north])
     count = counts_ref[row].astype(F32)
     zonal = (pairs, orders, parts, total_waves)
-    zonal_tables(zonal, count, sine, pair_ref, basis_ref, aux_ref, coarse_ref)
-
-    for copy in copies[3:]:
+    zonal_rows(zonal, count, sine, pair_ref, aux_ref)
+
+    for copy in copies[3:5]:
         copy.wait()
     for t, ref in enumerate((legendre_ref, slope_ref)):
         for s in range(pairs):
@@ -165,14 +207,21 @@
     both = [jnp.concatenate([a, b], axis=0).astype(BF16) for a, b in zip(plain, slope)]
     plain = [a.astype(BF16) for a in plain]
 
+    copies[5].wait()
+    operators = []
+    for g, f in enumerate(FIELD_OF):
+        padded = jnp.pad(ops_ref[f].astype(F32), ((0, LANES - levels), (0, 0)))
+        first = LANES - g * pad
+        moved = jnp.concatenate([padded[first:], padded[:first]], axis=0) if g else padded
+        operators.append(moved.astype(BF16))
+
+    for copy in copies[6:]:
+        copy.wait()
     sums = [[] for _ in range(FIELDS)]
     for f in range(fields):
-        field = spectral_ref[:, f].reshape(pairs * parts * width, levels)
-        vertical = dot(field, ops_ref[f], NT).astype(BF16)
         for c in range(parts):
             for s in range(pairs):
-                start = (s * parts + c) * width
-                block = vertical[start : start + width]
+                block = spectral_ref[s, f, c]
                 if f == 2:
                     result = dot(both[s], block)
                     sums[2].append(result[rows:])
@@ -180,9 +229,11 @@
                 else:
                     sums[f].append(dot(plain[s], block))
 
-    sums = [jnp.concatenate(x, axis=0) for x in sums]
-    sums = [jnp.pad(x, ((0, 0), (0, LANES - levels))) for x in sums]
-    sums = [pltpu.roll(x, g * pad, 1) if g else x for g, x in enumerate(sums)]
+    for g in range(FIELDS):
+        exact = jnp.concatenate(sums[g], axis=0)
+        high = exact.astype(BF16)
+        low = (exact - high.astype(F32)).astype(BF16)
+        sums[g] = dot(high, operators[g], NT) + dot(low, operators[g], NT)
     lane = iota(sums[0].shape, 1)
     south = jnp.where(rank * width < half, 1.0, -1.0)
     piece_rows = parts * sub
@@ -201,9 +252,20 @@
             send_ref[j * level_ranks + d] = own.astype(BF16)
             send_ref[(lats + j) * level_ranks + d] = (own * factor).astype(BF16)
 
-
-def grid_kernel(sizes, received_ref, basis_ref, aux_ref, out_hbm, out_ref, sent):
+    @pl.when(table_early())
+    def _():
+        zonal_table(sub, aux_ref, rows_ref, fine_ref, basis_ref)
+
+
+def grid_kernel(
+    sizes, received_ref, early_ref, aux_ref, out_hbm, basis_ref, out_ref, rows_ref, fine_ref, sent
+):
     level_ranks, levels_out, pad, group, total_waves = sizes
+
+    @pl.when(jnp.logical_not(table_early()))
+    def _():
+        zonal_table(group, aux_ref, rows_ref, fine_ref, basis_ref)
+
     chunks, chunk_rows, lanes = received_ref.shape
     sources = chunks // level_ranks
     data = received_ref[...].astype(F32).reshape(sources, level_ranks, chunk_rows, lanes)
@@ -216,23 +278,26 @@
     span = zonal.shape[1]
     imag = (iota(zonal.shape, 1) // group) % 2 == 1
     swapped = jnp.where(imag, pltpu.roll(zonal, group, 1), pltpu.roll(zonal, span - group, 1))
-    coeffs[3] = swapped * aux_ref[:1]
+    coeffs[3] = swapped * aux_ref[8:9]
+    coeffs[1] = coeffs[1] * (-1.0 / total_waves)
     coeffs = jnp.concatenate(coeffs, axis=0).astype(BF16)
 
-    inverse, count = aux_ref[8:9, :1], aux_ref[16:17, :1]
+    count = aux_ref[16:17, :LANES].astype(jnp.int32)
     copies = []
-    for start in range(0, NLON, COLS):
-        values = dot(coeffs, basis_ref[start : start + COLS], NT)
+    start = 0
+    for index, size in enumerate(COLUMNS):
+        values = dot(coeffs, basis_ref[start : start + size], NT)
         first, second, third, fourth = (values[g * keep : g * keep + levels_out] for g in range(4))
-        result = -(first * fourth * inverse + second * third * (1.0 / total_waves))
-        inside = (start + iota(result.shape, 1)).astype(F32) < count
-        window = (slice(None), slice(None), slice(start, start + COLS))
-        out_ref[:, 0, start : start + COLS] = jnp.where(inside, result, 0.0)
+        result = first * fourth + second * third
+        inside = start + iota((1, size), 1) < count[:, :1]
+        window = (slice(None), slice(None), slice(start, start + size))
+        out_ref[:, 0, start : start + size] = jnp.where(inside, result, 0.0)
         copy = pltpu.make_async_copy(
-            out_ref.at[window], out_hbm.at[window], sent.at[start // COLS]
+            out_ref.at[window], out_hbm.at[window], sent.at[index]
         )
         copy.start()
         copies.append(copy)
+        start += size
     for copy in copies:
         copy.wait()
 
@@ -259,6 +324,10 @@
     placed = pltpu.VMEM if resident else jax.ShapeDtypeStruct
     sources = [lon_counts, sine_lat, pair_map]
     sources += [legendre, legendre_slope, vertical_ops, by_position]
+    tables = [
+        pltpu.VMEM((3 + LANES // 32, 8, 2 * parts * slots), F32),
+        pltpu.VMEM((2, LANES, 2 * parts * slots), F32),
+    ]
     spaces = [pltpu.SMEM] * 3 + [pltpu.VMEM] * 4
     send, basis, aux = pl.pallas_call(
         functools.partial(front_kernel, (level_ranks, levels_out, pad, total_waves)),
@@ -273,7 +342,7 @@
         + [
             pltpu.VMEM((2 * group * lats, full), F32),
             pltpu.VMEM((level_ranks, parts * group * lats, LANES), F32),
-            pltpu.VMEM((2, NLON // LANES, 2 * parts * slots), F32),
+            *tables,
             pltpu.SemaphoreType.DMA((len(sources) - 1 + fields,)),
         ],
         name="front",
@@ -284,17 +353,23 @@
     )
     if resident:
         basis = pltpu.with_memory_space_constraint(basis, pltpu.VMEM)
-    return pl.pallas_call(
+    tendency, _ = pl.pallas_call(
         functools.partial(grid_kernel, (level_ranks, levels_out, pad, group, total_waves)),
-        out_shape=jax.ShapeDtypeStruct((levels_out, 1, NLON), F32),
+        out_shape=[
+            jax.ShapeDtypeStruct((levels_out, 1, NLON), F32),
+            placed((NLON, 2 * parts * slots), BF16),
+        ],
         in_specs=[vmem, vmem, vmem],
-        out_specs=hbm,
+        out_specs=[hbm, vmem],
+        input_output_aliases={1: 1},
         scratch_shapes=[
             pltpu.VMEM((levels_out, 1, NLON), F32),
-            pltpu.SemaphoreType.DMA((NLON // COLS,)),
+            *tables,
+            pltpu.SemaphoreType.DMA((len(COLUMNS),)),
         ],
         name="grid_tendency",
     )(received, basis, aux)
+    return tendency
 
 
 def solution(mesh):

time: 18.9 us -> 18.5 us (0.979)
  blocking collectives: 15.3 us -> 15 us
    all_to_all x1, blocking collectives: 15.3 us -> 15 us  [per_device(): lax.all_to_all(send, ('wave', 'lev'), split_axis=0, concat_axis=0, tiled=...]
where the time goes in v4:
time: 18.5 us; the launch traced here: 18.3 us
  blocking collectives  15 us (81%)
  Pallas kernels  3.31 us (18%)
    all_to_all x1, blocking collectives, per_device(): lax.all_to_all(send, ('wave', 'lev'), split_axis=0, concat_axis=0, tiled=...  15 us
    pallas_call x1, Pallas kernels, per_device(): pl.pallas_call(functools.partial(front_kernel, (level_ranks, levels_out,...  1.96 us
    pallas_call x1, Pallas kernels, per_device(): pl.pallas_call(functools.partial(grid_kernel, (level_ranks, levels_out, p...  1.34 us

profile of v4, /device:TPU:0, one launch (start us, length us, event | category | flops | bytes accessed | tf_op | source)
XLA Modules:
  0.0 18.3 jit_solution(10087071727363621382)
XLA Ops:
  0.0 2.0 %front.1 = (bf16[32,16,128]{2,1,0:T(8,128)(2,1)S(1)}, bf16[5120,128]{1,0:T(8,128)(2,1)S(1)}, f32[24,128]{1,0:T(8,128)S(1)}) custom-call(s32[8]{0:T(128)} %counts_hbm.1, f32[4]{0:T(128)} %sine_hbm.1, s32[32]{0:T(128)} %pair_hbm.1, bf16[4,2,4,192]{3,2,1,0:T(4,128)(2,1)} %legendre_hbm.1, bf16[4,2,4,192]{3,2,1,0:T(4,128)(2,1)} %slope_hbm.1, ...), custom_call_target="tpu_custom_call" | custom-call | tf_op jit(solution)/shard_map/front/pallas_call | solution.py:332
  2.0 15.0 %all_to_all.5.received_ref = bf16[32,16,128]{2,1,0:T(8,128)(2,1)S(1)} all-to-all(bf16[32,16,128]{2,1,0:T(8,128)(2,1)S(1)} %get-tuple-element.9), channel_id=1, replica_groups=mesh['wave'=8,'lev'=4] {'wave','lev'}, dimensions={0} | all-to-all | bytes 262144 | tf_op jit(solution)/shard_map/all_to_all | solution.py:350
  17.0 1.3 %grid_tendency.1 = (f32[18,1,5120]{2,1,0:T(1,128)}, bf16[5120,128]{1,0:T(8,128)(2,1)S(1)}) custom-call(bf16[32,16,128]{2,1,0:T(8,128)(2,1)S(1)} %all_to_all.5.received_ref, bf16[5120,128]{1,0:T(8,128)(2,1)S(1)} %get-tuple-element.10.early_ref, f32[24,128]{1,0:T(8,128)S(1)} %get-tuple-element.11.aux_ref), custom_call_target="tpu_custom_call", output_to_operand_aliasing={{1}: (1, {})} | custom-call | tf_op jit(solution)/shard_map/grid_tendency/pallas_call | solution.py:356

commit v5 on v4

--- a/solution.py
+++ b/solution.py
@@ -11,6 +11,8 @@
 NLON = 5120
 FIELDS = 4
 FIELD_OF = (0, 1, 2, 2)
+MAIN = 16
+REST = 2
 LANES = 128
 COLUMNS = (1280, 1280, 1280, 768, 512)
 RESIDENT = 4 << 20
@@ -52,22 +54,23 @@
 
 def zonal_rows(sizes, count, sine, pair_ref, aux_ref):
     pairs, orders, parts, total_waves = sizes
-    sub = pairs * orders
     shape = (8, aux_ref.shape[1])
+    sources = total_waves // 2 // pairs
     lane = iota(shape, 1)
-    slot = (lane // (parts * sub)) * pairs + (lane % sub) // orders
+    slot = (lane % sources) * pairs + (lane // (sources * orders)) % pairs
     number = jnp.zeros(shape, jnp.int32)
     for index in range(total_waves // 2):
         number = jnp.where(slot == index, pair_ref[index], number)
-    waves = jnp.where(lane % orders == 1, total_waves - 1 - number, number).astype(F32)
-    imag = (lane // sub) % parts
+    second = (lane // sources) % orders == 1
+    waves = jnp.where(second, total_waves - 1 - number, number).astype(F32)
+    imag = lane // (shape[1] // parts)
     scale = 1.0 / (1.0 - jnp.full(shape, sine * sine)) / total_waves
     aux_ref[:8] = waves
     aux_ref[8:16] = jnp.where(imag == 1, -waves, waves) * scale
     aux_ref[16:] = jnp.full(shape, count)
 
 
-def zonal_table(group, aux_ref, rows_ref, fine_ref, basis_ref):
+def zonal_table(aux_ref, rows_ref, fine_ref, basis_ref):
     waves, count = aux_ref[:8], aux_ref[16:]
     shape = waves.shape
     lanes = shape[1]
@@ -83,7 +86,7 @@
     cosine, sine_part = cos_sin(waves[:1] * (8 * index).astype(F32), count[:1], inverse[:1])
     rows_ref[3 : 3 + groups // 8] = cosine.reshape(groups // 8, 8, lanes)
     rows_ref[3 + groups // 8 :] = sine_part.reshape(groups // 8, 8, lanes)
-    imag = (iota(shape, 1) // group) % 2
+    imag = iota(shape, 1) // (lanes // 2)
     lower_cos, lower_sin = cos_sin(waves * iota(shape, 0).astype(F32), count, inverse, imag)
     for g in range(groups):
         upper = pl.ds(g % 8, 1)
@@ -140,12 +143,13 @@
     ops_ref,
     spectral_ref,
     table_ref,
-    joined_ref,
+    main_ref,
+    rest_ref,
     rows_ref,
     fine_ref,
     arrived,
 ):
-    level_ranks, levels_out, pad, total_waves = sizes
+    level_ranks, levels_out, total_waves = sizes
     pairs, fields, parts, width, levels = spectral_ref.shape
     _, orders, lats, full = legendre_ref.shape
     half = full // 2
@@ -169,6 +173,13 @@
     ]
     for copy in copies:
         copy.start()
+
+    rest = levels_out - min(levels_out, MAIN)
+    shape = (level_ranks * MAIN, levels)
+    r, level = iota(shape, 0), iota(shape, 1)
+    wanted = (r // MAIN) * levels_out + MAIN + r % REST
+    chosen = (level == wanted) & (r % REST < rest)
+    places = [(chosen & ((r % MAIN) // REST == g)).astype(F32).astype(BF16) for g in range(FIELDS)]
 
     for copy in copies[:3]:
         copy.wait()
@@ -207,15 +218,7 @@
     both = [jnp.concatenate([a, b], axis=0).astype(BF16) for a, b in zip(plain, slope)]
     plain = [a.astype(BF16) for a in plain]
 
-    copies[5].wait()
-    operators = []
-    for g, f in enumerate(FIELD_OF):
-        padded = jnp.pad(ops_ref[f].astype(F32), ((0, LANES - levels), (0, 0)))
-        first = LANES - g * pad
-        moved = jnp.concatenate([padded[first:], padded[:first]], axis=0) if g else padded
-        operators.append(moved.astype(BF16))
-
-    for copy in copies[6:]:
+    for copy in copies[5:]:
         copy.wait()
     sums = [[] for _ in range(FIELDS)]
     for f in range(fields):
@@ -224,77 +227,144 @@
                 block = spectral_ref[s, f, c]
                 if f == 2:
                     result = dot(both[s], block)
-                    sums[2].append(result[rows:])
-                    sums[3].append(result[:rows])
+                    sums[3].append(result[rows:])
+                    sums[2].append(result[:rows])
                 else:
                     sums[f].append(dot(plain[s], block))
+
+    operators = []
+    for g, f in enumerate(FIELD_OF):
+        below = LANES - levels - g * MAIN
+        pieces = [ops_ref[f], jnp.zeros((below, levels), BF16)]
+        if g:
+            pieces = [jnp.zeros((g * MAIN, levels), BF16)] + pieces
+        if rest:
+            pieces.append(dot(places[g], ops_ref[f]).astype(BF16))
+            pieces.append(jnp.zeros((LANES - level_ranks * MAIN, levels), BF16))
+        operators.append(jnp.concatenate(pieces, axis=0))
 
     for g in range(FIELDS):
         exact = jnp.concatenate(sums[g], axis=0)
         high = exact.astype(BF16)
         low = (exact - high.astype(F32)).astype(BF16)
         sums[g] = dot(high, operators[g], NT) + dot(low, operators[g], NT)
-    lane = iota(sums[0].shape, 1)
+    count_rows = pairs * rows
+    lane = iota((parts * count_rows, LANES), 1)
+    right = lane[:count_rows] >= LANES // parts
     south = jnp.where(rank * width < half, 1.0, -1.0)
-    piece_rows = parts * sub
-    factor = jnp.where(iota((piece_rows, LANES), 1) // pad == 2, -south, south)
+    factor = jnp.where((iota((sub, LANES), 1) // MAIN) % FIELDS == FIELDS - 1, -south, south)
     for d in range(level_ranks):
         shift = d * levels_out
-        lane_field = ((lane + (LANES - shift)) % LANES) // pad
-        joined = sums[FIELDS - 1]
-        for g in range(FIELDS - 1):
-            joined = jnp.where(lane_field == g, sums[g], joined)
+        joined = sums[0][:, :LANES]
+        for g in range(1, FIELDS):
+            joined = jnp.where(lane >= shift + g * MAIN, sums[g][:, :LANES], joined)
+        real, imag = joined[:count_rows], joined[count_rows:]
         if shift:
-            joined = pltpu.roll(joined, LANES - shift, 1)
-        joined_ref[d] = joined
+            real = pltpu.roll(real, LANES - shift, 1)
+        imag = pltpu.roll(imag, (LANES // parts - shift) % LANES, 1)
+        main_ref[d] = jnp.where(right, imag, real)
         for j in range(lats):
-            own = joined_ref[d, pl.ds(j, piece_rows, stride=lats), :]
-            send_ref[j * level_ranks + d] = own.astype(BF16)
-            send_ref[(lats + j) * level_ranks + d] = (own * factor).astype(BF16)
+            own = main_ref[d, pl.ds(j, sub, stride=lats), :]
+            shape = (sub // 2, 2, LANES)
+            for place, piece in ((j, own), (lats + j, own * factor)):
+                send_ref[place * level_ranks + d, : sub // 2] = piece.astype(BF16).reshape(shape)
+    if rest:
+        block = MAIN
+        total = (sums[0] + sums[1] + sums[2] + sums[3])[:, LANES:]
+        total = total[:count_rows] + pltpu.roll(total[count_rows:], FIELDS * REST, 1)
+        pieces = [total[s * rows : (s + 1) * rows] for s in range(pairs)]
+        pieces = [pltpu.roll(x, s * block, 1) if s else x for s, x in enumerate(pieces)]
+        lane = iota((rows, LANES), 1)
+        lane_field = (iota((orders, LANES), 1) // REST) % FIELDS
+        factor = jnp.where(lane_field == FIELDS - 1, -south, south)
+        for d in range(level_ranks):
+            joined = pieces[0]
+            for s in range(1, pairs):
+                joined = jnp.where(lane >= (d + s) * block, pieces[s], joined)
+            if d:
+                joined = pltpu.roll(joined, LANES - d * block, 1)
+            rest_ref[d] = joined
+            for j in range(lats):
+                own = rest_ref[d, pl.ds(j, orders, stride=lats), :]
+                for place, piece in ((j, own), (lats + j, own * factor)):
+                    send_ref[place * level_ranks + d, sub // 2] = piece.astype(BF16)
 
     @pl.when(table_early())
     def _():
-        zonal_table(sub, aux_ref, rows_ref, fine_ref, basis_ref)
+        zonal_table(aux_ref, rows_ref, fine_ref, basis_ref)
 
 
 def grid_kernel(
-    sizes, received_ref, early_ref, aux_ref, out_hbm, basis_ref, out_ref, rows_ref, fine_ref, sent
+    sizes,
+    received_ref,
+    early_ref,
+    aux_ref,
+    out_hbm,
+    basis_ref,
+    out_ref,
+    main_ref,
+    rest_ref,
+    rows_ref,
+    fine_ref,
+    sent,
 ):
-    level_ranks, levels_out, pad, group, total_waves = sizes
+    level_ranks, levels_out, pairs, orders, total_waves = sizes
+    sub = pairs * orders
+    main_levels = min(levels_out, MAIN)
+    rest = levels_out - main_levels
 
     @pl.when(jnp.logical_not(table_early()))
     def _():
-        zonal_table(group, aux_ref, rows_ref, fine_ref, basis_ref)
-
-    chunks, chunk_rows, lanes = received_ref.shape
-    sources = chunks // level_ranks
-    data = received_ref[...].astype(F32).reshape(sources, level_ranks, chunk_rows, lanes)
-    total = jnp.sum(data, axis=1)
-
-    by_level = total.reshape(sources * chunk_rows, lanes).T
-    keep = -(-levels_out // 8) * 8
-    coeffs = [by_level[g * pad : g * pad + keep] for g in range(FIELDS)]
-    zonal = coeffs[3]
-    span = zonal.shape[1]
-    imag = (iota(zonal.shape, 1) // group) % 2 == 1
-    swapped = jnp.where(imag, pltpu.roll(zonal, group, 1), pltpu.roll(zonal, span - group, 1))
-    coeffs[3] = swapped * aux_ref[8:9]
-    coeffs[1] = coeffs[1] * (-1.0 / total_waves)
-    coeffs = jnp.concatenate(coeffs, axis=0).astype(BF16)
-
-    count = aux_ref[16:17, :LANES].astype(jnp.int32)
+        zonal_table(aux_ref, rows_ref, fine_ref, basis_ref)
+
+    sources = received_ref.shape[0] // level_ranks
+    half = sub * sources
+    derivative = aux_ref[8:9]
+    scale = -1.0 / total_waves
+    if rest:
+        for a in range(sources):
+            parts = [received_ref[a * level_ranks + b, sub // 2] for b in range(level_ranks)]
+            rest_ref[orders * a : orders * (a + 1)] = sum(x.astype(F32) for x in parts)
+        stacked = [rest_ref[pl.ds(w, sources, stride=orders), :] for w in range(orders)]
+        turned = jnp.concatenate(stacked, axis=0).T
+        block = FIELDS * REST
+        pieces = [
+            turned[s * MAIN + c * block : s * MAIN + (c + 1) * block]
+            for c in range(2)
+            for s in range(pairs)
+        ]
+        extra = jnp.concatenate(pieces, axis=1)
+        field = iota(extra.shape, 0) // REST
+        swapped = pltpu.roll(extra, half, 1) * derivative
+        extra = jnp.where(field == 2, swapped, jnp.where(field == 1, extra * scale, extra))
+    for a in range(sources):
+        parts = [received_ref[a * level_ranks + b, : sub // 2] for b in range(level_ranks)]
+        main_ref[sub * a : sub * (a + 1)] = sum(x.astype(F32) for x in parts).reshape(sub, LANES)
+    stacked = [main_ref[pl.ds(i, sources, stride=sub), :] for i in range(sub)]
+    turned = jnp.concatenate(stacked, axis=0).T
+    coeffs = jnp.concatenate([turned[: LANES // 2], turned[LANES // 2 :]], axis=1)
+    coeffs = [coeffs[g * MAIN : (g + 1) * MAIN] for g in range(FIELDS)]
+    coeffs[2] = pltpu.roll(coeffs[2], half, 1) * derivative
+    coeffs[1] = coeffs[1] * scale
+    coeffs = jnp.concatenate(coeffs + ([extra] if rest else []), axis=0).astype(BF16)
+
+    count = aux_ref[16:17, :1].astype(jnp.int32)
     copies = []
     start = 0
     for index, size in enumerate(COLUMNS):
         values = dot(coeffs, basis_ref[start : start + size], NT)
-        first, second, third, fourth = (values[g * keep : g * keep + levels_out] for g in range(4))
-        result = first * fourth + second * third
-        inside = start + iota((1, size), 1) < count[:, :1]
+        inside = start + iota((1, size), 1) < count
+        first, second, third, slope = (values[g * MAIN : (g + 1) * MAIN] for g in range(FIELDS))
+        result = jnp.where(inside, first * third + second * slope, 0.0)
+        out_ref[:main_levels, 0, start : start + size] = result[:main_levels]
+        if rest:
+            value = values[FIELDS * MAIN :]
+            product = value * pltpu.roll(value, 2 * REST, 0)
+            result = product[:REST] + product[REST : 2 * REST]
+            result = jnp.where(inside, result, 0.0)
+            out_ref[main_levels:, 0, start : start + size] = result[:rest]
         window = (slice(None), slice(None), slice(start, start + size))
-        out_ref[:, 0, start : start + size] = jnp.where(inside, result, 0.0)
-        copy = pltpu.make_async_copy(
-            out_ref.at[window], out_hbm.at[window], sent.at[index]
-        )
+        copy = pltpu.make_async_copy(out_ref.at[window], out_hbm.at[window], sent.at[index])
         copy.start()
         copies.append(copy)
         start += size
@@ -309,12 +379,14 @@
     slots = pair_map.shape[0]
     total_waves = 2 * slots
     levels_out = levels // level_ranks
-    pad = LANES // FIELDS
     lats, full = legendre.shape[2:]
     orders = legendre.shape[1]
     group = pairs * orders
     assert rows == 2 * lats == lon_counts.shape[0]
-    assert levels_out <= pad and levels <= LANES
+    rest = max(levels_out - MAIN, 0)
+    assert rest <= REST and levels + FIELDS * MAIN - MAIN <= LANES
+    assert parts * FIELDS * MAIN == LANES and group % 2 == 0
+    assert not rest or level_ranks + pairs - 1 <= LANES // MAIN
     assert (full // 2) % width == 0
 
     vmem = pl.BlockSpec(memory_space=pltpu.VMEM)
@@ -330,9 +402,9 @@
     ]
     spaces = [pltpu.SMEM] * 3 + [pltpu.VMEM] * 4
     send, basis, aux = pl.pallas_call(
-        functools.partial(front_kernel, (level_ranks, levels_out, pad, total_waves)),
+        functools.partial(front_kernel, (level_ranks, levels_out, total_waves)),
         out_shape=[
-            pltpu.VMEM((rows * level_ranks, parts * group, LANES), BF16),
+            pltpu.VMEM((rows * level_ranks, group // 2 + (rest > 0), 2, LANES), BF16),
             placed((NLON, 2 * parts * slots), BF16),
             pltpu.VMEM((24, 2 * parts * slots), F32),
         ],
@@ -341,7 +413,8 @@
         scratch_shapes=[space(x.shape, x.dtype) for space, x in zip(spaces, sources)]
         + [
             pltpu.VMEM((2 * group * lats, full), F32),
-            pltpu.VMEM((level_ranks, parts * group * lats, LANES), F32),
+            pltpu.VMEM((level_ranks, group * lats, LANES), F32),
+            pltpu.VMEM((level_ranks, orders * lats, LANES), F32),
             *tables,
             pltpu.SemaphoreType.DMA((len(sources) - 1 + fields,)),
         ],
@@ -354,7 +427,7 @@
     if resident:
         basis = pltpu.with_memory_space_constraint(basis, pltpu.VMEM)
     tendency, _ = pl.pallas_call(
-        functools.partial(grid_kernel, (level_ranks, levels_out, pad, group, total_waves)),
+        functools.partial(grid_kernel, (level_ranks, levels_out, pairs, orders, total_waves)),
         out_shape=[
             jax.ShapeDtypeStruct((levels_out, 1, NLON), F32),
             placed((NLON, 2 * parts * slots), BF16),
@@ -364,6 +437,8 @@
         input_output_aliases={1: 1},
         scratch_shapes=[
             pltpu.VMEM((levels_out, 1, NLON), F32),
+            pltpu.VMEM((rows * group, LANES), F32),
+            pltpu.VMEM((rows * orders, LANES), F32),
             *tables,
             pltpu.SemaphoreType.DMA((len(COLUMNS),)),
         ],

time: 18.5 us -> 18.3 us (0.989)
  blocking collectives: 15 us -> 14.4 us
  Pallas kernels: 3.31 us -> 3.73 us
    all_to_all x1, blocking collectives: 15 us -> 14.4 us  [per_device(): lax.all_to_all(send, ('wave', 'lev'), split_axis=0, concat_axis=0, tiled=...]
    pallas_call x1, Pallas kernels: 1.96 us -> 2.25 us  [per_device(): pl.pallas_call(functools.partial(front_kernel, (level_ranks, levels_out,...]
where the time goes in v5:
time: 18.3 us; the launch traced here: 18.1 us
  blocking collectives  14.4 us (79%)
  Pallas kernels  3.73 us (20%)
    all_to_all x1, blocking collectives, per_device(): lax.all_to_all(send, ('wave', 'lev'), split_axis=0, concat_axis=0, tiled=...  14.4 us
    pallas_call x1, Pallas kernels, per_device(): pl.pallas_call(functools.partial(front_kernel, (level_ranks, levels_out,...  2.25 us
    pallas_call x1, Pallas kernels, per_device(): pl.pallas_call(functools.partial(grid_kernel, (level_ranks, levels_out, p...  1.49 us

profile of v5, /device:TPU:0, one launch (start us, length us, event | category | flops | bytes accessed | tf_op | source)
XLA Modules:
  0.0 18.1 jit_solution(7814665370654519449)
XLA Ops:
  0.0 2.2 %front.1 = (bf16[32,5,2,128]{3,2,1,0:T(2,128)(2,1)S(1)}, bf16[5120,128]{1,0:T(8,128)(2,1)S(1)}, f32[24,128]{1,0:T(8,128)S(1)}) custom-call(s32[8]{0:T(128)} %counts_hbm.1, f32[4]{0:T(128)} %sine_hbm.1, s32[32]{0:T(128)} %pair_hbm.1, bf16[4,2,4,192]{3,2,1,0:T(4,128)(2,1)} %legendre_hbm.1, bf16[4,2,4,192]{3,2,1,0:T(4,128)(2,1)} %slope_hbm.1, ...), custom_call_target="tpu_custom_call" | custom-call | tf_op jit(solution)/shard_map/front/pallas_call | solution.py:404
  2.3 14.4 %all_to_all.5.received_ref = bf16[32,5,2,128]{3,2,1,0:T(2,128)(2,1)S(1)} all-to-all(bf16[32,5,2,128]{3,2,1,0:T(2,128)(2,1)S(1)} %get-tuple-element.9), channel_id=1, replica_groups=mesh['wave'=8,'lev'=4] {'wave','lev'}, dimensions={0} | all-to-all | bytes 163840 | tf_op jit(solution)/shard_map/all_to_all | solution.py:423
  16.6 1.5 %grid_tendency.1 = (f32[18,1,5120]{2,1,0:T(1,128)}, bf16[5120,128]{1,0:T(8,128)(2,1)S(1)}) custom-call(bf16[32,5,2,128]{3,2,1,0:T(2,128)(2,1)S(1)} %all_to_all.5.received_ref, bf16[5120,128]{1,0:T(8,128)(2,1)S(1)} %get-tuple-element.10.early_ref, f32[24,128]{1,0:T(8,128)S(1)} %get-tuple-element.11.aux_ref), custom_call_target="tpu_custom_call", output_to_operand_aliasing={{1}: (1, {})} | custom-call | tf_op jit(solution)/shard_map/grid_tendency/pallas_call | solution.py:429

commit v6 on v5

--- a/solution.py
+++ b/solution.py
@@ -168,7 +168,7 @@
                 (slope_hbm, slope_ref),
                 (ops_hbm, ops_ref),
             ]
-            + [(spectral_hbm.at[:, f], spectral_ref.at[:, f]) for f in range(fields)]
+            + [(spectral_hbm, spectral_ref)]
         )
     ]
     for copy in copies:
@@ -247,7 +247,8 @@
         exact = jnp.concatenate(sums[g], axis=0)
         high = exact.astype(BF16)
         low = (exact - high.astype(F32)).astype(BF16)
-        sums[g] = dot(high, operators[g], NT) + dot(low, operators[g], NT)
+        both_terms = dot(jnp.concatenate([high, low], axis=0), operators[g], NT)
+        sums[g] = both_terms[: exact.shape[0]] + both_terms[exact.shape[0] :]
     count_rows = pairs * rows
     lane = iota((parts * count_rows, LANES), 1)
     right = lane[:count_rows] >= LANES // parts
@@ -416,7 +417,7 @@
             pltpu.VMEM((level_ranks, group * lats, LANES), F32),
             pltpu.VMEM((level_ranks, orders * lats, LANES), F32),
             *tables,
-            pltpu.SemaphoreType.DMA((len(sources) - 1 + fields,)),
+            pltpu.SemaphoreType.DMA((len(sources),)),
         ],
         name="front",
     )(*sources)

time: 18.3 us -> 18.2 us (level)
  no operation moved by 1% of the time
where the time goes in v6:
time: 18.2 us; the launch traced here: 18 us
  blocking collectives  14.4 us (79%)
  Pallas kernels  3.58 us (20%)
    all_to_all x1, blocking collectives, per_device(): lax.all_to_all(send, ('wave', 'lev'), split_axis=0, concat_axis=0, tiled=...  14.4 us
    pallas_call x1, Pallas kernels, per_device(): pl.pallas_call(functools.partial(front_kernel, (level_ranks, levels_out,...  2.09 us
    pallas_call x1, Pallas kernels, per_device(): pl.pallas_call(functools.partial(grid_kernel, (level_ranks, levels_out, p...  1.49 us

profile of v6, /device:TPU:0, one launch (start us, length us, event | category | flops | bytes accessed | tf_op | source)
XLA Modules:
  0.0 18.0 jit_solution(14593406429699087665)
XLA Ops:
  0.0 2.1 %front.1 = (bf16[32,5,2,128]{3,2,1,0:T(2,128)(2,1)S(1)}, bf16[5120,128]{1,0:T(8,128)(2,1)S(1)}, f32[24,128]{1,0:T(8,128)S(1)}) custom-call(s32[8]{0:T(128)} %counts_hbm.1, f32[4]{0:T(128)} %sine_hbm.1, s32[32]{0:T(128)} %pair_hbm.1, bf16[4,2,4,192]{3,2,1,0:T(4,128)(2,1)} %legendre_hbm.1, bf16[4,2,4,192]{3,2,1,0:T(4,128)(2,1)} %slope_hbm.1, ...), custom_call_target="tpu_custom_call" | custom-call | tf_op jit(solution)/shard_map/front/pallas_call | solution.py:405
  2.1 14.4 %all_to_all.5.received_ref = bf16[32,5,2,128]{3,2,1,0:T(2,128)(2,1)S(1)} all-to-all(bf16[32,5,2,128]{3,2,1,0:T(2,128)(2,1)S(1)} %get-tuple-element.9), channel_id=1, replica_groups=mesh['wave'=8,'lev'=4] {'wave','lev'}, dimensions={0} | all-to-all | bytes 163840 | tf_op jit(solution)/shard_map/all_to_all | solution.py:424
  16.5 1.5 %grid_tendency.1 = (f32[18,1,5120]{2,1,0:T(1,128)}, bf16[5120,128]{1,0:T(8,128)(2,1)S(1)}) custom-call(bf16[32,5,2,128]{3,2,1,0:T(2,128)(2,1)S(1)} %all_to_all.5.received_ref, bf16[5120,128]{1,0:T(8,128)(2,1)S(1)} %get-tuple-element.10.early_ref, f32[24,128]{1,0:T(8,128)S(1)} %get-tuple-element.11.aux_ref), custom_call_target="tpu_custom_call", output_to_operand_aliasing={{1}: (1, {})} | custom-call | tf_op jit(solution)/shard_map/grid_tendency/pallas_call | solution.py:430

commit v7 on v6

--- a/solution.py
+++ b/solution.py
@@ -301,22 +301,34 @@
     early_ref,
     aux_ref,
     out_hbm,
-    basis_ref,
     out_ref,
     main_ref,
     rest_ref,
     rows_ref,
     fine_ref,
+    late_ref,
     sent,
+):
+    refs = (out_hbm, out_ref, main_ref, rest_ref, sent)
+    early = table_early()
+
+    @pl.when(early)
+    def _():
+        grid_step(sizes, received_ref, early_ref, aux_ref, *refs)
+
+    @pl.when(jnp.logical_not(early))
+    def _():
+        zonal_table(aux_ref, rows_ref, fine_ref, late_ref)
+        grid_step(sizes, received_ref, late_ref, aux_ref, *refs)
+
+
+def grid_step(
+    sizes, received_ref, basis_ref, aux_ref, out_hbm, out_ref, main_ref, rest_ref, sent
 ):
     level_ranks, levels_out, pairs, orders, total_waves = sizes
     sub = pairs * orders
     main_levels = min(levels_out, MAIN)
     rest = levels_out - main_levels
-
-    @pl.when(jnp.logical_not(table_early()))
-    def _():
-        zonal_table(aux_ref, rows_ref, fine_ref, basis_ref)
 
     sources = received_ref.shape[0] // level_ranks
     half = sub * sources
@@ -427,25 +439,21 @@
     )
     if resident:
         basis = pltpu.with_memory_space_constraint(basis, pltpu.VMEM)
-    tendency, _ = pl.pallas_call(
+    return pl.pallas_call(
         functools.partial(grid_kernel, (level_ranks, levels_out, pairs, orders, total_waves)),
-        out_shape=[
-            jax.ShapeDtypeStruct((levels_out, 1, NLON), F32),
-            placed((NLON, 2 * parts * slots), BF16),
-        ],
+        out_shape=jax.ShapeDtypeStruct((levels_out, 1, NLON), F32),
         in_specs=[vmem, vmem, vmem],
-        out_specs=[hbm, vmem],
-        input_output_aliases={1: 1},
+        out_specs=hbm,
         scratch_shapes=[
             pltpu.VMEM((levels_out, 1, NLON), F32),
             pltpu.VMEM((rows * group, LANES), F32),
             pltpu.VMEM((rows * orders, LANES), F32),
             *tables,
+            pltpu.VMEM((NLON, 2 * parts * slots), BF16),
             pltpu.SemaphoreType.DMA((len(COLUMNS),)),
         ],
         name="grid_tendency",
     )(received, basis, aux)
-    return tendency
 
 
 def solution(mesh):

time: 18.2 us -> 18.2 us (level)
  no operation moved by 1% of the time
where the time goes in v7:
time: 18.2 us; the launch traced here: 18 us
  blocking collectives  14.4 us (79%)
  Pallas kernels  3.58 us (20%)
    all_to_all x1, blocking collectives, per_device(): lax.all_to_all(send, ('wave', 'lev'), split_axis=0, concat_axis=0, tiled=...  14.4 us
    pallas_call x1, Pallas kernels, per_device(): pl.pallas_call(functools.partial(front_kernel, (level_ranks, levels_out,...  2.09 us
    pallas_call x1, Pallas kernels, per_device(): pl.pallas_call(functools.partial(grid_kernel, (level_ranks, levels_out, p...  1.49 us

profile of v7, /device:TPU:0, one launch (start us, length us, event | category | flops | bytes accessed | tf_op | source)
XLA Modules:
  0.0 18.0 jit_solution(4321485969028414675)
XLA Ops:
  0.0 2.1 %front.1 = (bf16[32,5,2,128]{3,2,1,0:T(2,128)(2,1)S(1)}, bf16[5120,128]{1,0:T(8,128)(2,1)S(1)}, f32[24,128]{1,0:T(8,128)S(1)}) custom-call(s32[8]{0:T(128)} %counts_hbm.1, f32[4]{0:T(128)} %sine_hbm.1, s32[32]{0:T(128)} %pair_hbm.1, bf16[4,2,4,192]{3,2,1,0:T(4,128)(2,1)} %legendre_hbm.1, bf16[4,2,4,192]{3,2,1,0:T(4,128)(2,1)} %slope_hbm.1, ...), custom_call_target="tpu_custom_call" | custom-call | tf_op jit(solution)/shard_map/front/pallas_call | solution.py:417
  2.1 14.4 %all_to_all.5.received_ref = bf16[32,5,2,128]{3,2,1,0:T(2,128)(2,1)S(1)} all-to-all(bf16[32,5,2,128]{3,2,1,0:T(2,128)(2,1)S(1)} %get-tuple-element.8), channel_id=1, replica_groups=mesh['wave'=8,'lev'=4] {'wave','lev'}, dimensions={0} | all-to-all | bytes 163840 | tf_op jit(solution)/shard_map/all_to_all | solution.py:436
  16.5 1.5 %grid_tendency.1 = f32[18,1,5120]{2,1,0:T(1,128)} custom-call(bf16[32,5,2,128]{3,2,1,0:T(2,128)(2,1)S(1)} %all_to_all.5.received_ref, bf16[5120,128]{1,0:T(8,128)(2,1)S(1)} %get-tuple-element.9.early_ref, f32[24,128]{1,0:T(8,128)S(1)} %get-tuple-element.10.aux_ref), custom_call_target="tpu_custom_call" | custom-call | tf_op jit(solution)/shard_map/grid_tendency/pallas_call | solution.py:442
